TPU v7x, 32 devices: a whole 2x2x4 slice. The times are simulated.
32 devices in a mesh: patch: 2 (over y), exp: 4 (over z), strip: 2 (over x), band: 2 (over core).
Axes of the slice: x: 2, y: 2, z: 4, core: 2. Of those that a mesh axis runs over, the one named last changes fastest.
Arguments:
- images: float32 [64, 64, 512], P(('patch', 'exp'), 'strip', 'band'), parts along dimension 0, may hold values from -80 to 80
- valid_mask: int32 [64, 64, 512], P(('patch', 'exp'), 'strip', 'band'), parts along dimension 0, may hold values from 0 to 1, as said below
- basis_index: int32 [64, 4, 2], P(('patch', 'exp'), 'strip'), parts along dimension 0, may hold values from 0 to 15
- match_index: int32 [64, 4, 2], P(('patch', 'exp'), 'strip'), parts along dimension 0, may hold values from 0 to 15
- psf_bank: float32 [16, 81], replicated, may hold values from 0.05 to 1
Outputs:
- coadd_image: float32 [128, 512], P(('patch', 'strip'), 'band'), parts along dimension 0
- difference: float32 [64, 64, 512], P(('patch', 'exp'), 'strip', 'band'), parts along dimension 0
There are 2 independent parts, one for each index of `patch`. A program takes and returns all parts, laid end to end along the dimension named above; an argument that names none is the same for every part. Nothing has to cross between parts.
Inputs may be any that keep to these rules, and one draw needn't show every extreme that they name: `valid_mask`: one marks a valid pixel of that exposure.
All inputs are finite; a program needn't handle non-finite values.
Results may differ from a plain program's by a relative error of at most 0.0003.
Values sent between devices are 32-bit elements; how exact they have to be, the bound alone decides.
No kernel may reach another device: no remote copies, remote signals or barrier semaphores. Data moves between devices by JAX's collectives and lax.ppermute only.
A program may use at most 128 MiB of HBM per device.

v0:
```python
import jax
import jax.numpy as jnp
from jax import lax
from jax.sharding import PartitionSpec as P

TILE_ROWS = 16
KERNEL = 9


sentinel = 1e30


def extended(cells, sides, width):
    for axis, dim in sides:
        count = lax.axis_size(axis)
        ends = count - 1
        head = lax.slice_in_dim(cells, 0, width, axis=dim)
        tail = lax.slice_in_dim(cells, cells.shape[dim] - width, cells.shape[dim], axis=dim)
        cells = jnp.concatenate(
            [
                lax.ppermute(tail, axis, [(i, (i + 1) % count) for i in range(ends)]),
                cells,
                lax.ppermute(head, axis, [((i + 1) % count, i) for i in range(ends)]),
            ],
            axis=dim,
        )
    return cells


def joined(value, axis, join):
    pieces = jax.tree.map(lambda part: lax.all_gather(part, axis), value)
    head = jax.tree.map(lambda part: part[0], pieces)
    tail = jax.tree.map(lambda part: part[1:], pieces)
    total, _ = lax.scan(lambda total, section: (join(total, section), None), head, tail)
    return total


def vary_conv(padded, kernels, blend_map):
    row_count = kernels.shape[-3]
    col_count = blend_map.shape[0]
    low_acc = jnp.zeros(kernels.shape[:-2] + (col_count,), jnp.float32)
    high_acc = jnp.zeros(kernels.shape[:-2] + (col_count,), jnp.float32)
    for row_off in range(KERNEL):
        for col_off in range(KERNEL):
            window = padded[..., row_off : row_off + row_count, col_off : col_off + col_count]
            tap_at = row_off * KERNEL + col_off
            low_acc = low_acc + kernels[..., 0, tap_at][..., None] * window
            high_acc = high_acc + kernels[..., 1, tap_at][..., None] * window
    return (1.0 - blend_map) * low_acc + blend_map * high_acc


def tile_kernels(tile_index, psf_bank):
    normed = psf_bank / jnp.sum(psf_bank, axis=1, keepdims=True)
    onehot = (tile_index[..., None] == jnp.arange(psf_bank.shape[0], dtype=jnp.int32)).astype(
        jnp.float32
    )
    kernels = jnp.einsum("etkb,bq->etkq", onehot, normed, precision=lax.Precision.HIGHEST)
    return jnp.repeat(kernels, TILE_ROWS, axis=1)


def member(stacked, position):
    return lax.index_in_dim(stacked, position, axis=stacked.ndim - 3, keepdims=False)


def lower_three(first_set, second_set):
    a_zero, a_one, a_two = (member(first_set, 0), member(first_set, 1), member(first_set, 2))
    b_zero, b_one, b_two = (member(second_set, 0), member(second_set, 1), member(second_set, 2))
    first = jnp.minimum(a_zero, b_zero)
    second = jnp.minimum(jnp.minimum(a_one, b_one), jnp.maximum(a_zero, b_zero))
    third = jnp.minimum(
        jnp.minimum(a_two, b_two),
        jnp.minimum(jnp.maximum(a_one, b_zero), jnp.maximum(a_zero, b_one)),
    )
    return jnp.stack([first, second, third], axis=-3)


def upper_three(first_set, second_set):
    a_zero, a_one, a_two = (member(first_set, 0), member(first_set, 1), member(first_set, 2))
    b_zero, b_one, b_two = (member(second_set, 0), member(second_set, 1), member(second_set, 2))
    first = jnp.maximum(a_zero, b_zero)
    second = jnp.maximum(jnp.maximum(a_one, b_one), jnp.minimum(a_zero, b_zero))
    third = jnp.maximum(
        jnp.maximum(a_two, b_two),
        jnp.maximum(jnp.minimum(a_one, b_zero), jnp.minimum(a_zero, b_one)),
    )
    return jnp.stack([first, second, third], axis=-3)


def combine(left_stats, right_stats):
    return (
        left_stats[0] + right_stats[0],
        left_stats[1] + right_stats[1],
        lower_three(left_stats[2], right_stats[2]),
        upper_three(left_stats[3], right_stats[3]),
    )


def tree_fold(statistics):
    while statistics[0].shape[0] > 1:
        length_now = statistics[0].shape[0]
        split_at = length_now // 2
        front_part = tuple((entry[:split_at] for entry in statistics))
        back_part = tuple((entry[split_at : 2 * split_at] for entry in statistics))
        merged = combine(front_part, back_part)
        statistics = merged
    return tuple((entry[0] for entry in statistics))


def finish(statistics):
    total_sum = statistics[0]
    valid_count = statistics[1]
    low_three, high_three = (statistics[2], statistics[3])
    low_sum = member(low_three, 0) + member(low_three, 1) + member(low_three, 2)
    high_sum = member(high_three, 0) + member(high_three, 1) + member(high_three, 2)
    return (total_sum - low_sum - high_sum) / (valid_count - 6.0)


def on_device(images, valid_mask, basis_index, match_index, psf_bank):
    rim_width = KERNEL // 2
    col_count = images.shape[2]
    columns = lax.axis_index("band") * col_count + jnp.arange(col_count, dtype=jnp.int32)
    blend_map = columns.astype(jnp.float32) / (col_count * lax.axis_size("band") - 1)
    image_padded = extended(images, (("strip", 1), ("band", 2)), rim_width)
    warped = vary_conv(image_padded, tile_kernels(basis_index, psf_bank), blend_map)
    is_valid = valid_mask == 1
    filler = jnp.full(warped.shape, sentinel, jnp.float32)
    low_start = jnp.stack([jnp.where(is_valid, warped, sentinel), filler, filler], axis=1)
    high_start = jnp.stack([jnp.where(is_valid, warped, -sentinel), -filler, -filler], axis=1)
    local_stats = tree_fold(
        (jnp.where(is_valid, warped, 0.0), valid_mask.astype(jnp.float32), low_start, high_start)
    )
    total_stats = joined(local_stats, "exp", combine)
    coadd_image = finish(total_stats)
    coadd_padded = extended(coadd_image, (("strip", 0), ("band", 1)), rim_width)
    matched = vary_conv(coadd_padded, tile_kernels(match_index, psf_bank), blend_map)
    return (coadd_image, images - matched)


def solution(mesh):
    return jax.shard_map(
        on_device,
        mesh=mesh,
        in_specs=(
            P(("patch", "exp"), "strip", "band"),
            P(("patch", "exp"), "strip", "band"),
            P(("patch", "exp"), "strip", None),
            P(("patch", "exp"), "strip", None),
            P(),
        ),
        out_specs=(P(("patch", "strip"), "band"), P(("patch", "exp"), "strip", "band")),
        check_vma=False,
    )
```

profile of v0, /device:TPU:0, one launch (start us, length us, event | category | flops | bytes accessed | tf_op | source)
XLA Modules:
  0.0 134.8 jit_solution(10140037247067433031)
XLA Ops:
  1.5 4.9 %collective-permute-start = (f32[8,4,256]{2,1,0:T(4,128)S(1)}, f32[8,4,256]{2,1,0:T(4,128)S(1)}, u32[]{:S(2)}, u32[]{:S(2)}) collective-permute-start(f32[8,4,256]{2,1,0:T(4,128)S(1)} %get-tuple-element.428), channel_id=1, source_target_pairs={{0,2},{1,3},{4,6},{5,7},{8,10},{9,11},{12,14},{13,15},{16,18},{17,... | collective-permute-start | bytes 98312 | tf_op jit(solution)/shard_map/ppermute | solution.py:21
  10.8 1.4 %slice_reduce_fusion.195 = (f32[8,32]{1,0:T(8,128)S(1)}, f32[8,32]{1,0:T(8,128)S(1)}, f32[8,32]{1,0:T(8,128)S(1)}, f32[8,32]{1,0:T(8,128)S(1)}, f32[8,32]{1,0:T(...) fusion(f32[8,32,2,81]{3,1,2,0:T(8,128)S(1)} %bitcast.96), kind=kLoop, calls=%fused_computation.230 | loop fusion | bytes 38912 | tf_op jit(solution)/shard_map/slice | solution.py:48
  12.2 1.4 %slice_reduce_fusion.318 = (f32[8,32]{1,0:T(8,128)S(1)}, f32[8,32]{1,0:T(8,128)S(1)}, f32[8,32]{1,0:T(8,128)S(1)}, f32[8,32]{1,0:T(8,128)S(1)}, f32[8,32]{1,0:T(...) fusion(f32[8,32,2,81]{3,1,2,0:T(8,128)S(1)} %bitcast.97), kind=kLoop, calls=%fused_computation.353 | loop fusion | bytes 38912 | tf_op jit(solution)/shard_map/slice | solution.py:47
  13.6 1.4 %slice_reduce_fusion.319 = (f32[8,32]{1,0:T(8,128)S(1)}, f32[8,32]{1,0:T(8,128)S(1)}, f32[8,32]{1,0:T(8,128)S(1)}, f32[8,32]{1,0:T(8,128)S(1)}, f32[8,32]{1,0:T(...) fusion(f32[8,32,2,81]{3,1,2,0:T(8,128)S(1)} %bitcast.98), kind=kLoop, calls=%fused_computation.354 | loop fusion | bytes 38912 | tf_op jit(solution)/shard_map/slice | solution.py:47
  15.0 1.4 %slice_reduce_fusion.320 = (f32[8,32]{1,0:T(8,128)S(1)}, f32[8,32]{1,0:T(8,128)S(1)}, f32[8,32]{1,0:T(8,128)S(1)}, f32[8,32]{1,0:T(8,128)S(1)}, f32[8,32]{1,0:T(...) fusion(f32[8,32,2,81]{3,1,2,0:T(8,128)S(1)} %bitcast.99), kind=kLoop, calls=%fused_computation.355 | loop fusion | bytes 38912 | tf_op jit(solution)/shard_map/slice | solution.py:47
  16.4 1.4 %slice_reduce_fusion.321 = (f32[8,32]{1,0:T(8,128)S(1)}, f32[8,32]{1,0:T(8,128)S(1)}, f32[8,32]{1,0:T(8,128)S(1)}, f32[8,32]{1,0:T(8,128)S(1)}, f32[8,32]{1,0:T(...) fusion(f32[8,32,2,81]{3,1,2,0:T(8,128)S(1)} %bitcast.100), kind=kLoop, calls=%fused_computation.356 | loop fusion | bytes 38912 | tf_op jit(solution)/shard_map/slice | solution.py:47
  17.7 1.4 %slice_reduce_fusion.322 = (f32[8,32]{1,0:T(8,128)S(1)}, f32[8,32]{1,0:T(8,128)S(1)}, f32[8,32]{1,0:T(8,128)S(1)}, f32[8,32]{1,0:T(8,128)S(1)}, f32[8,32]{1,0:T(...) fusion(f32[8,32,2,81]{3,1,2,0:T(8,128)S(1)} %bitcast.101), kind=kLoop, calls=%fused_computation.357 | loop fusion | bytes 38912 | tf_op jit(solution)/shard_map/slice | solution.py:47
  21.9 1.5 %slice_reduce_fusion.33 = (f32[8,32]{1,0:T(8,128)S(1)}, f32[8,32]{1,0:T(8,128)S(1)}, f32[8,32]{1,0:T(8,128)S(1)}, f32[8,32]{1,0:T(8,128)S(1)}, f32[8,32]{1,0:T(8...) fusion(f32[8,32,2,81]{3,1,2,0:T(8,128)S(1)} %bitcast.86), kind=kLoop, calls=%fused_computation.66 | loop fusion | bytes 38912 | tf_op jit(solution)/shard_map/slice | solution.py:48
  23.4 1.4 %slice_reduce_fusion.156 = (f32[8,32]{1,0:T(8,128)S(1)}, f32[8,32]{1,0:T(8,128)S(1)}, f32[8,32]{1,0:T(8,128)S(1)}, f32[8,32]{1,0:T(8,128)S(1)}, f32[8,32]{1,0:T(...) fusion(f32[8,32,2,81]{3,1,2,0:T(8,128)S(1)} %bitcast.87), kind=kLoop, calls=%fused_computation.189 | loop fusion | bytes 38912 | tf_op jit(solution)/shard_map/slice | solution.py:47
  24.8 1.4 %slice_reduce_fusion.157 = (f32[8,32]{1,0:T(8,128)S(1)}, f32[8,32]{1,0:T(8,128)S(1)}, f32[8,32]{1,0:T(8,128)S(1)}, f32[8,32]{1,0:T(8,128)S(1)}, f32[8,32]{1,0:T(...) fusion(f32[8,32,2,81]{3,1,2,0:T(8,128)S(1)} %bitcast.88), kind=kLoop, calls=%fused_computation.190 | loop fusion | bytes 38912 | tf_op jit(solution)/shard_map/slice | solution.py:47
  26.2 1.4 %slice_reduce_fusion.158 = (f32[8,32]{1,0:T(8,128)S(1)}, f32[8,32]{1,0:T(8,128)S(1)}, f32[8,32]{1,0:T(8,128)S(1)}, f32[8,32]{1,0:T(8,128)S(1)}, f32[8,32]{1,0:T(...) fusion(f32[8,32,2,81]{3,1,2,0:T(8,128)S(1)} %bitcast.89), kind=kLoop, calls=%fused_computation.191 | loop fusion | bytes 38912 | tf_op jit(solution)/shard_map/slice | solution.py:47
  27.6 1.4 %slice_reduce_fusion.159 = (f32[8,32]{1,0:T(8,128)S(1)}, f32[8,32]{1,0:T(8,128)S(1)}, f32[8,32]{1,0:T(8,128)S(1)}, f32[8,32]{1,0:T(8,128)S(1)}, f32[8,32]{1,0:T(...) fusion(f32[8,32,2,81]{3,1,2,0:T(8,128)S(1)} %bitcast.90), kind=kLoop, calls=%fused_computation.192 | loop fusion | bytes 38912 | tf_op jit(solution)/shard_map/slice | solution.py:47
  29.0 1.4 %slice_reduce_fusion.160 = (f32[8,32]{1,0:T(8,128)S(1)}, f32[8,32]{1,0:T(8,128)S(1)}, f32[8,32]{1,0:T(8,128)S(1)}, f32[8,32]{1,0:T(8,128)S(1)}, f32[8,32]{1,0:T(...) fusion(f32[8,32,2,81]{3,1,2,0:T(8,128)S(1)} %bitcast.91), kind=kLoop, calls=%fused_computation.193 | loop fusion | bytes 38912 | tf_op jit(solution)/shard_map/slice | solution.py:47
  32.8 13.6 %all_gather.13 = f32[4,32,256]{2,1,0:T(8,128)S(1)} all-gather(f32[1,32,256]{2,1,0:T(8,128)S(1)} %slice_add_fusion.4), channel_id=1, replica_groups=mesh['patch'=2,'exp'=4,'strip'=2,'band'=2] {'exp'}, dimensions={0}, use_global_device_ids=true | all-gather | bytes 163840 | tf_op jit(solution)/shard_map/all_gather | solution.py:31
  49.8 2.0 %collective-permute-done.3 = f32[8,40,4]{2,1,0:T(8,128)S(1)} collective-permute-done((f32[8,40,4]{2,1,0:T(8,128)S(1)}, f32[8,40,4]{2,1,0:T(8,128)S(1)}, u32[]{:S(2)}, u32[]{:S(2)}) %collective-permute-start.3) | collective-permute-done | bytes 5152 | tf_op jit(solution)/shard_map/ppermute | solution.py:23
  52.1 11.3 %broadcast_select_fusion = (f32[8,32,256]{2,1,0:T(8,128)S(1)}, f32[8,32,256]{2,1,0:T(8,128)S(1)}, pred[8,32,256]{2,1,0:T(8,128)(4,1)S(1)}) fusion(f32[8,32]{1,0:T(8,128)S(1)} %get-tuple-element.347, f32[8,32]{1,0:T(8,128)S(1)} %get-tuple-element.348, f32[8,32]{1,0:T(8,128)S(1)} %get-tuple-element.349, f32[8,32]{1,0:T(8,128)S(1)} %get-tuple-element.350, ...), kind=kLoop, calls=%fused_computation.361 | loop fusion | flops 21692416 | bytes 21237760 | tf_op jit(solution)/shard_map/jit(_where)/select_n | solution.py:128
  63.5 14.9 %all_gather.15 = f32[4,3,32,256]{3,2,1,0:T(8,128)S(1)} all-gather(f32[1,3,32,256]{3,2,1,0:T(8,128)S(1)} %pad_maximum_fusion.6), channel_id=1, replica_groups=mesh['patch'=2,'exp'=4,'strip'=2,'band'=2] {'exp'}, dimensions={0}, use_global_device_ids=true | all-gather | bytes 491520 | tf_op jit(solution)/shard_map/all_gather | solution.py:31
  79.2 13.7 %all_gather.12 = f32[4,32,256]{2,1,0:T(8,128)S(1)} all-gather(f32[1,32,256]{2,1,0:T(8,128)S(1)} %slice_add_fusion.5), channel_id=1, replica_groups=mesh['patch'=2,'exp'=4,'strip'=2,'band'=2] {'exp'}, dimensions={0}, use_global_device_ids=true | all-gather | bytes 163840 | tf_op jit(solution)/shard_map/all_gather | solution.py:31
  93.7 15.1 %all_gather.14 = f32[4,3,32,256]{3,2,1,0:T(8,128)S(1)} all-gather(f32[1,3,32,256]{3,2,1,0:T(8,128)S(1)} %pad_maximum_fusion.5), channel_id=1, replica_groups=mesh['patch'=2,'exp'=4,'strip'=2,'band'=2] {'exp'}, dimensions={0}, use_global_device_ids=true | all-gather | bytes 491520 | tf_op jit(solution)/shard_map/all_gather | solution.py:31
  110.2 4.5 %collective-permute-start.4 = (f32[4,256]{1,0:T(4,128)S(1)}, f32[4,256]{1,0:T(4,128)S(1)}, u32[]{:S(2)}, u32[]{:S(2)}) collective-permute-start(f32[4,256]{1,0:T(4,128)S(1)} %get-tuple-element.526), channel_id=1, source_target_pairs={{0,2},{1,3},{4,6},{5,7},{8,10},{9,11},{12,14},{13,15},{16,18},{17,... | collective-permute-start | bytes 12296 | tf_op jit(solution)/shard_map/ppermute | solution.py:21
  114.7 1.5 %collective-permute-start.5 = (f32[4,256]{1,0:T(4,128)S(1)}, f32[4,256]{1,0:T(4,128)S(1)}, u32[]{:S(2)}, u32[]{:S(2)}) collective-permute-start(f32[4,256]{1,0:T(4,128)S(1)} %get-tuple-element.527), channel_id=1, source_target_pairs={{2,0},{3,1},{6,4},{7,5},{10,8},{11,9},{14,12},{15,13},{18,16},{19,... | collective-permute-start | bytes 12296 | tf_op jit(solution)/shard_map/ppermute | solution.py:23
  117.3 2.9 %collective-permute-done.5 = f32[4,256]{1,0:T(4,128)S(1)} collective-permute-done((f32[4,256]{1,0:T(4,128)S(1)}, f32[4,256]{1,0:T(4,128)S(1)}, u32[]{:S(2)}, u32[]{:S(2)}) %collective-permute-start.5) | collective-permute-done | bytes 4128 | tf_op jit(solution)/shard_map/ppermute | solution.py:23
  122.9 1.7 %collective-permute-done.7 = f32[40,4]{1,0:T(8,128)S(1)} collective-permute-done((f32[40,4]{1,0:T(8,128)S(1)}, f32[40,4]{1,0:T(8,128)S(1)}, u32[]{:S(2)}, u32[]{:S(2)}) %collective-permute-start.7) | collective-permute-done | bytes 672 | tf_op jit(solution)/shard_map/ppermute | solution.py:23
  125.6 9.2 %add_subtract_fusion = f32[8,32,256]{2,1,0:T(8,128)} fusion(f32[8,32,256]{2,1,0:T(8,128)S(1)} %copy-done, f32[8,32]{1,0:T(8,128)S(1)} %get-tuple-element.185, f32[8,32]{1,0:T(8,128)S(1)} %get-tuple-element.186, f32[8,32]{1,0:T(8,128)S(1)} %get-tuple-element.187, f32[8,32]{1,0:T(8,128)S(1)} %get-tuple-element.188, f32[8,32]{1,0:T(8,128)S(1)} %get-tuple-element.189, ...), kind=kLoop, calls=%fused_computation.31 | loop fusion | flops 21364736 | bytes 3346432 | tf_op jit(solution)/shard_map/sub | solution.py:136
  (98 shorter events, 21.8 us)
Async XLA Ops:
  0.6 7.1 %copy-start.6 = (f32[16,81]{1,0:T(8,128)S(1)}, f32[16,81]{1,0:T(8,128)}, u32[]{:S(2)}) copy-start(f32[16,81]{1,0:T(8,128)} %param.11) | copy-start | bytes 15556
  1.5 45.5 %collective-permute-start = (f32[8,4,256]{2,1,0:T(4,128)S(1)}, f32[8,4,256]{2,1,0:T(4,128)S(1)}, u32[]{:S(2)}, u32[]{:S(2)}) collective-permute-start(f32[8,4,256]{2,1,0:T(4,128)S(1)} %get-tuple-element.428), channel_id=1, source_target_pairs={{0,2},{1,3},{4,6},{5,7},{8,10},{9,11},{12,14},{13,15},{16,18},{17,... | collective-permute-start | bytes 98312 | tf_op jit(solution)/shard_map/ppermute | solution.py:21
  6.4 40.6 %collective-permute-start.1 = (f32[8,4,256]{2,1,0:T(4,128)S(1)}, f32[8,4,256]{2,1,0:T(4,128)S(1)}, u32[]{:S(2)}, u32[]{:S(2)}) collective-permute-start(f32[8,4,256]{2,1,0:T(4,128)S(1)} %get-tuple-element.429), channel_id=1, source_target_pairs={{2,0},{3,1},{6,4},{7,5},{10,8},{11,9},{14,12},{15,13},{18,16},{19,... | collective-permute-start | bytes 98312 | tf_op jit(solution)/shard_map/ppermute | solution.py:23
  7.7 0.7 copy-start.7
  19.1 1.4 %copy-start.8 = (s32[8,2,2]{0,2,1:T(2,128)S(1)}, s32[8,2,2]{0,2,1:T(2,128)}, u32[]{:S(2)}) copy-start(s32[8,2,2]{0,2,1:T(2,128)} %param.10) | copy-start | bytes 388
  30.3 1.4 %copy-start = (f32[8,32,256]{2,1,0:T(8,128)S(1)}, f32[8,32,256]{2,1,0:T(8,128)}, u32[]{:S(2)}) copy-start(f32[8,32,256]{2,1,0:T(8,128)} %param.7) | copy-start | bytes 786436
  31.7 1.0 copy-start.2
  46.4 0.7 copy-start.4
  47.2 2.6 %collective-permute-start.2 = (f32[8,40,4]{2,1,0:T(8,128)S(1)}, f32[8,40,4]{2,1,0:T(8,128)S(1)}, u32[]{:S(2)}, u32[]{:S(2)}) collective-permute-start(f32[8,40,4]{2,1,0:T(8,128)S(1)} %get-tuple-element.416), channel_id=1, source_target_pairs={{0,1},{2,3},{4,5},{6,7},{8,9},{10,11},{12,13},{14,15},{16,17},{18,... | collective-permute-start | bytes 15368 | tf_op jit(solution)/shard_map/ppermute | solution.py:21
  48.5 3.3 %collective-permute-start.3 = (f32[8,40,4]{2,1,0:T(8,128)S(1)}, f32[8,40,4]{2,1,0:T(8,128)S(1)}, u32[]{:S(2)}, u32[]{:S(2)}) collective-permute-start(f32[8,40,4]{2,1,0:T(8,128)S(1)} %get-tuple-element.417), channel_id=1, source_target_pairs={{1,0},{3,2},{5,4},{7,6},{9,8},{11,10},{13,12},{15,14},{17,16},{19,... | collective-permute-start | bytes 15368 | tf_op jit(solution)/shard_map/ppermute | solution.py:23
  78.4 0.7 copy-start.1
  92.9 0.7 copy-start.5
  108.8 1.0 slice-start
  108.8 1.0 slice-start.1
  108.8 1.0 slice-start.2
  110.2 15.4 %copy-start.3 = (f32[32,256]{1,0:T(8,128)}, f32[32,256]{1,0:T(8,128)S(1)}, u32[]{:S(2)}) copy-start(f32[32,256]{1,0:T(8,128)S(1)} %fusion.19) | copy-start | bytes 98308
  110.2 7.1 %collective-permute-start.4 = (f32[4,256]{1,0:T(4,128)S(1)}, f32[4,256]{1,0:T(4,128)S(1)}, u32[]{:S(2)}, u32[]{:S(2)}) collective-permute-start(f32[4,256]{1,0:T(4,128)S(1)} %get-tuple-element.526), channel_id=1, source_target_pairs={{0,2},{1,3},{4,6},{5,7},{8,10},{9,11},{12,14},{13,15},{16,18},{17,... | collective-permute-start | bytes 12296 | tf_op jit(solution)/shard_map/ppermute | solution.py:21
  114.7 5.5 %collective-permute-start.5 = (f32[4,256]{1,0:T(4,128)S(1)}, f32[4,256]{1,0:T(4,128)S(1)}, u32[]{:S(2)}, u32[]{:S(2)}) collective-permute-start(f32[4,256]{1,0:T(4,128)S(1)} %get-tuple-element.527), channel_id=1, source_target_pairs={{2,0},{3,1},{6,4},{7,5},{10,8},{11,9},{14,12},{15,13},{18,16},{19,... | collective-permute-start | bytes 12296 | tf_op jit(solution)/shard_map/ppermute | solution.py:23
  120.3 2.6 %collective-permute-start.6 = (f32[40,4]{1,0:T(8,128)S(1)}, f32[40,4]{1,0:T(8,128)S(1)}, u32[]{:S(2)}, u32[]{:S(2)}) collective-permute-start(f32[40,4]{1,0:T(8,128)S(1)} %get-tuple-element.512), channel_id=1, source_target_pairs={{0,1},{2,3},{4,5},{6,7},{8,9},{10,11},{12,13},{14,15},{16,17},{18,... | collective-permute-start | bytes 1928 | tf_op jit(solution)/shard_map/ppermute | solution.py:21
  121.6 3.1 %collective-permute-start.7 = (f32[40,4]{1,0:T(8,128)S(1)}, f32[40,4]{1,0:T(8,128)S(1)}, u32[]{:S(2)}, u32[]{:S(2)}) collective-permute-start(f32[40,4]{1,0:T(8,128)S(1)} %get-tuple-element.513), channel_id=1, source_target_pairs={{1,0},{3,2},{5,4},{7,6},{9,8},{11,10},{13,12},{15,14},{17,16},{19,... | collective-permute-start | bytes 1928 | tf_op jit(solution)/shard_map/ppermute | solution.py:23
where the time goes:
time: 135 us
  blocking collectives  57.3 us (42%)
  local copies, waits for them, and re-layouts  30.3 us (22%)
  other arithmetic  21.6 us (16%)
  starting transfers between devices  17.3 us (13%)
  waiting for transfers between devices  6.63 us (5%)
    all_gather x4, blocking collectives, joined(): pieces = jax.tree.map(lambda part: lax.all_gather(part, axis), value)  57.3 us
    slice x14, local copies, waits for them, and re-layouts, vary_conv(): low_acc = low_acc + kernels[..., 0, tap_at][..., None] * window  18.6 us
    ppermute x4, starting transfers between devices, extended(): lax.ppermute(tail, axis, [(i, (i + 1) % count) for i in range(ends)])  11.9 us
    select_n x1, other arithmetic, on_device(): jnp.where(is_valid, warped, -sentinel)  11.3 us
    sub x1, other arithmetic, on_device(): return (coadd_image, images - matched)  9.24 us
    ppermute x4, waiting for transfers between devices, extended(): lax.ppermute(head, axis, [((i + 1) % count, i) for i in range(ends)])  6.62 us
    ppermute x4, starting transfers between devices, extended(): lax.ppermute(head, axis, [((i + 1) % count, i) for i in range(ends)])  5.39 us
    slice x4, local copies, waits for them, and re-layouts, vary_conv(): high_acc = high_acc + kernels[..., 1, tap_at][..., None] * window  5.15 us
  transfers between devices with their start and end apart: 8, of which 3 were waited for; matrix products, arithmetic and copies ran while one was open for 18% of the time, Pallas kernels for 0%

commit v1 on v0

v1 whole, which is shorter than its diff:
```python
import functools

import jax
import jax.numpy as jnp
from jax import lax
from jax.experimental import pallas as pl
from jax.experimental.pallas import tpu as pltpu
from jax.sharding import PartitionSpec as P

TILE_ROWS = 16
KERNEL = 9
RIM = KERNEL // 2
SLOTS = TILE_ROWS + 2 * RIM
LANES = 128
DEPTH = 256
SENTINEL = 1.0e30
LIMIT = 1.0e29

VMEM = pl.BlockSpec(memory_space=pltpu.VMEM)
SMEM = pl.BlockSpec(memory_space=pltpu.SMEM)


def call(body, outs, specs, flops, size):
    single = not isinstance(outs, (list, tuple))
    return pl.pallas_call(
        body,
        out_shape=outs,
        in_specs=specs,
        out_specs=VMEM if single else [VMEM] * len(outs),
        compiler_params=pltpu.CompilerParams(vmem_limit_bytes=12 << 20),
        cost_estimate=pl.CostEstimate(flops=flops, bytes_accessed=size, transcendentals=0),
    )


def iota(shape, dim):
    return lax.broadcasted_iota(jnp.int32, shape, dim)


def split(value):
    high = value.astype(jnp.bfloat16)
    low = (value - high.astype(jnp.float32)).astype(jnp.bfloat16)
    return high, low


def blend_row(col_count):
    columns = lax.axis_index("band") * col_count + iota((1, col_count), 1)
    return columns.astype(jnp.float32) / float(col_count * lax.axis_size("band") - 1)


def tap_body(bank_ref, out_ref):
    bank = bank_ref[...]
    normed = bank / jnp.sum(bank, axis=1, keepdims=True)
    tap = iota((KERNEL * KERNEL, DEPTH), 0)
    row_off = (tap * 57) >> 9
    col_off = tap - row_off * KERNEL
    place = (iota((KERNEL * KERNEL, DEPTH), 1) == col_off * SLOTS + row_off).astype(jnp.float32)
    first = jnp.dot(normed, place, precision=lax.Precision.HIGHEST, preferred_element_type=jnp.float32)
    lane = iota((TILE_ROWS, DEPTH), 1)
    slot = lane - SLOTS * ((lane * 2731) >> 16)
    for base in range(bank.shape[0]):
        spread = jnp.broadcast_to(first[base : base + 1], (TILE_ROWS, DEPTH))
        rows = pltpu.roll(spread, 0, 1, stride=1, stride_axis=0)
        wrapped = jnp.where(slot < SLOTS - RIM, pltpu.roll(rows, DEPTH - RIM, 1), pltpu.roll(rows, SLOTS - RIM, 1))
        high, low = split(wrapped)
        out_ref[base, :TILE_ROWS, :] = high
        out_ref[base, TILE_ROWS:, :] = low


def shifted(rows):
    width = rows.shape[1]
    cols = width - LANES
    parts = []
    for col_off in range(KERNEL):
        amount = (RIM - col_off) % width
        moved = rows if amount == 0 else pltpu.roll(rows, amount, 1)
        parts.append(moved[:, :cols])
    parts.append(jnp.zeros((DEPTH - KERNEL * SLOTS, cols), jnp.float32))
    return split(jnp.concatenate(parts, axis=0))


def edge(first, last, has_first, has_last, lane):
    return jnp.where((lane < RIM) & has_first, first, 0.0) + jnp.where((lane >= LANES - RIM) & has_last, last, 0.0)


def sides():
    strip = lax.axis_index("strip")
    band = lax.axis_index("band")
    return (
        strip > 0,
        strip < lax.axis_size("strip") - 1,
        band > 0,
        band < lax.axis_size("band") - 1,
    )


def pack_body(swap_rows, swap_cols, images_ref, *outs):
    count, rows, cols = images_ref.shape
    above, below, left, right = sides()
    sub = iota((8, cols), 0)
    lane = iota((rows, LANES), 1)
    ups, downs = [], []
    for pair in range(count // 2):
        head = [images_ref[2 * pair + k, 0:8, :] for k in range(2)]
        tail = [images_ref[2 * pair + k, rows - 8 : rows, :] for k in range(2)]
        ups.append(jnp.where(sub < RIM, head[0], pltpu.roll(head[1], RIM, 0)))
        downs.append(jnp.where(sub < RIM, pltpu.roll(tail[0], RIM, 0), tail[1]))
    lefts = jnp.zeros((rows, LANES), jnp.float32)
    rights = jnp.zeros((rows, LANES), jnp.float32)
    for e in range(count):
        here = (lane >= RIM * e) & (lane < RIM * (e + 1))
        lefts = jnp.where(here, pltpu.roll(images_ref[e, :, :LANES], RIM * e, 1) if e else images_ref[e, :, :LANES], lefts)
        rights = jnp.where(here, pltpu.roll(images_ref[e, :, cols - LANES :], (RIM * (e + 1)) % LANES, 1), rights)
    outs = list(outs)
    if swap_rows:
        out = outs.pop(0)
        for pair in range(count // 2):
            out[8 * pair : 8 * pair + 8, :] = jnp.where(below, downs[pair], ups[pair])
    else:
        up, down = outs.pop(0), outs.pop(0)
        for pair in range(count // 2):
            up[8 * pair : 8 * pair + 8, :] = ups[pair]
            down[8 * pair : 8 * pair + 8, :] = downs[pair]
    if swap_cols:
        edges = [jnp.where(right, rights, lefts)]
    else:
        edges = [lefts, rights]
    for value in edges:
        outs.pop(0)[...] = value
    for value in edges:
        if swap_rows:
            outs.pop(0)[...] = jnp.where(below, value[rows - 8 :], value[:8])
        else:
            outs.pop(0)[...] = value[:8]
            outs.pop(0)[...] = value[rows - 8 :]


def warp_body(
    sent, images_ref, mask_ref, index_ref, taps_ref, above_ref, below_ref, left_ref, right_ref, c_al, c_ar, c_bl, c_br, out_ref
):
    count, rows, cols = images_ref.shape
    tiles = rows // TILE_ROWS
    above, below, left, right = sides()
    parity = (lax.axis_index("exp") + lax.axis_index("strip")) % 2
    tile = (1 - parity) if sent else parity
    start = pl.multiple_of(tile * TILE_ROWS, TILE_ROWS)
    prior = pl.multiple_of(jnp.maximum(start - 8, 0), 8)
    after = pl.multiple_of(jnp.minimum(start + TILE_ROWS, rows - 8), 8)
    top = tile == 0
    end = tile == tiles - 1
    sub = iota((8, cols), 0)
    sub_l = iota((8, LANES), 0)
    lane_l = iota((8, LANES), 1)
    lane_m = iota((TILE_ROWS, LANES), 1)
    blend = blend_row(cols)

    def put(first, last, e, lane):
        first = pltpu.roll(first, (LANES - RIM * e) % LANES, 1) if e else first
        last = pltpu.roll(last, (LANES - RIM - RIM * e) % LANES, 1)
        return edge(first, last, right, left, lane)

    rim_first = jnp.where(
        sub_l < RIM,
        jnp.where(end, jnp.where(below, c_br[...], 0.0), right_ref[pl.ds(after, 8), :]),
        jnp.where(top, jnp.where(above, c_ar[...], 0.0), right_ref[pl.ds(prior, 8), :]),
    )
    rim_last = jnp.where(
        sub_l < RIM,
        jnp.where(end, jnp.where(below, c_bl[...], 0.0), left_ref[pl.ds(after, 8), :]),
        jnp.where(top, jnp.where(above, c_al[...], 0.0), left_ref[pl.ds(prior, 8), :]),
    )
    main_first = right_ref[pl.ds(start, TILE_ROWS), :]
    main_last = left_ref[pl.ds(start, TILE_ROWS), :]
    for e in range(count):
        group = 8 * (e // 2)
        low_rows = below_ref[group : group + 8, :]
        high_rows = above_ref[group : group + 8, :]
        if e % 2:
            low_rows = pltpu.roll(low_rows, RIM, 0)
        else:
            high_rows = pltpu.roll(high_rows, RIM, 0)
        rim = jnp.where(
            sub < RIM,
            jnp.where(end, jnp.where(below, low_rows, 0.0), images_ref[e, pl.ds(after, 8), :]),
            jnp.where(top, jnp.where(above, high_rows, 0.0), images_ref[e, pl.ds(prior, 8), :]),
        )
        body = jnp.concatenate([images_ref[e, pl.ds(start, TILE_ROWS), :], rim], axis=0)
        edges = jnp.concatenate([put(main_first, main_last, e, lane_m), put(rim_first, rim_last, e, lane_l)], axis=0)
        high, low = shifted(jnp.concatenate([body, edges], axis=1))
        taps = jnp.concatenate([taps_ref[index_ref[e, tile, 0]], taps_ref[index_ref[e, tile, 1]]], axis=0)
        sums = jnp.dot(taps, high, preferred_element_type=jnp.float32) + jnp.dot(taps, low, preferred_element_type=jnp.float32)
        n = TILE_ROWS
        first = sums[0:n] + sums[n : 2 * n]
        second = sums[2 * n : 3 * n] + sums[3 * n : 4 * n]
        warped = (1.0 - blend) * first + blend * second
        out_ref[e] = jnp.where(mask_ref[e, pl.ds(start, TILE_ROWS), :] == 1, warped, SENTINEL)


def insert_low(three, value):
    a, b, c = three
    over = jnp.maximum(a, value)
    a = jnp.minimum(a, value)
    more = jnp.maximum(b, over)
    b = jnp.minimum(b, over)
    return a, b, jnp.minimum(c, more)


def insert_high(three, value):
    a, b, c = three
    under = jnp.minimum(a, value)
    a = jnp.maximum(a, value)
    less = jnp.minimum(b, under)
    b = jnp.maximum(b, under)
    return a, b, jnp.maximum(c, less)


def gather_body(own_ref, other_ref, out_ref):
    count, rows, cols = own_ref.shape
    big = jnp.full((8, LANES), SENTINEL, jnp.float32)
    for r in range(0, rows, 8):
        for c in range(0, cols, LANES):
            total = jnp.zeros((8, LANES), jnp.float32)
            number = jnp.zeros((8, LANES), jnp.float32)
            low, high = (big, big, big), (-big, -big, -big)
            for ref in (own_ref, other_ref):
                for e in range(count):
                    value = ref[e, r : r + 8, c : c + LANES]
                    valid = value < LIMIT
                    total = total + jnp.where(valid, value, 0.0)
                    number = number + jnp.where(valid, 1.0, 0.0)
                    low = insert_low(low, value)
                    high = insert_high(high, jnp.where(valid, value, -SENTINEL))
            for k, plane in enumerate((total, number) + low + high):
                out_ref[k, r : r + 8, c : c + LANES] = plane


def merge_low(a, b):
    return (
        jnp.minimum(a[0], b[0]),
        jnp.minimum(jnp.minimum(a[1], b[1]), jnp.maximum(a[0], b[0])),
        jnp.minimum(jnp.minimum(a[2], b[2]), jnp.minimum(jnp.maximum(a[1], b[0]), jnp.maximum(a[0], b[1]))),
    )


def merge_high(a, b):
    return (
        jnp.maximum(a[0], b[0]),
        jnp.maximum(jnp.maximum(a[1], b[1]), jnp.minimum(a[0], b[0])),
        jnp.maximum(jnp.maximum(a[2], b[2]), jnp.maximum(jnp.minimum(a[1], b[0]), jnp.minimum(a[0], b[1]))),
    )


def merge_body(last, own_ref, other_ref, out_ref):
    _, rows, cols = own_ref.shape
    for r in range(0, rows, 8):
        for c in range(0, cols, LANES):
            a = [own_ref[k, r : r + 8, c : c + LANES] for k in range(8)]
            b = [other_ref[k, r : r + 8, c : c + LANES] for k in range(8)]
            total, number = a[0] + b[0], a[1] + b[1]
            low = merge_low(a[2:5], b[2:5])
            high = merge_high(a[5:8], b[5:8])
            if last:
                low_sum = low[0] + low[1] + low[2]
                high_sum = high[0] + high[1] + high[2]
                out_ref[r : r + 8, c : c + LANES] = (total - low_sum - high_sum) / (number - 6.0)
            else:
                for k, plane in enumerate((total, number) + low + high):
                    out_ref[k, r : r + 8, c : c + LANES] = plane


def join_body(swap_cols, own_ref, pair_ref, a_same, a_cross, b_same, b_cross, coadd_ref, rim_ref, *outs):
    above, below, left, right = sides()
    parity = (lax.axis_index("exp") + lax.axis_index("strip")) % 2
    even = parity == 0
    own, pair = own_ref[...], pair_ref[...]
    n, cols = own.shape
    coadd_ref[:n, :] = jnp.where(even, own, pair)
    coadd_ref[n:, :] = jnp.where(even, pair, own)
    sub = iota((8, cols), 0)
    low = jnp.where(even, b_cross[:8, :], b_same[:8, :])
    high = jnp.where(even, a_same[n - 8 :, :], a_cross[n - 8 :, :])
    rim_ref[...] = jnp.where(sub < RIM, jnp.where(below, low, 0.0), jnp.where(above, high, 0.0))
    for ref, at in ((coadd_ref, 0), (rim_ref, 2 * n)):
        rows = ref.shape[0]
        lefts, rights = ref[:, :LANES], ref[:, cols - LANES :]
        if swap_cols:
            outs[0][at : at + rows, :] = jnp.where(right, rights, lefts)
        else:
            outs[0][at : at + rows, :] = lefts
            outs[1][at : at + rows, :] = rights


def match_body(images_ref, index_ref, taps_ref, coadd_ref, rim_ref, left_ref, right_ref, out_ref):
    count, rows, cols = images_ref.shape
    tiles = rows // TILE_ROWS
    _, _, left, right = sides()
    blend = blend_row(cols)
    sub = iota((8, cols), 0)
    lane = iota((rows + 8, LANES), 1)
    sub_l = iota((8, LANES), 0)
    edges = edge(right_ref[...], left_ref[...], right, left, lane)
    n = TILE_ROWS
    for tile in range(tiles):
        start = tile * n

        def rims(main, last, at):
            low = last if tile == tiles - 1 else main[start + n : start + n + 8]
            high = last if tile == 0 else main[start - 8 : start]
            return jnp.concatenate([main[start : start + n], jnp.where(at < RIM, low, high)], axis=0)

        body = rims(coadd_ref[...], rim_ref[...], sub)
        side = rims(edges[:rows], edges[rows:], sub_l)
        high, low = shifted(jnp.concatenate([body, side], axis=1))
        taps = jnp.concatenate([taps_ref[index_ref[e, tile, k]] for e in range(count) for k in range(2)], axis=0)
        sums = jnp.dot(taps, high, preferred_element_type=jnp.float32) + jnp.dot(taps, low, preferred_element_type=jnp.float32)
        for e in range(count):
            at = 4 * n * e
            first = sums[at : at + n] + sums[at + n : at + 2 * n]
            second = sums[at + 2 * n : at + 3 * n] + sums[at + 3 * n : at + 4 * n]
            out_ref[e, start : start + n, :] = images_ref[e, start : start + n, :] - (
                (1.0 - blend) * first + blend * second
            )


def moved(value, exp_bit, strip_step, band_step):
    sizes = [lax.axis_size(a) for a in ("exp", "strip", "band")]
    pairs = []
    for z in range(sizes[0]):
        for s in range(sizes[1]):
            for b in range(sizes[2]):
                s_from, b_from = s + strip_step, b + band_step
                if sizes[1] == 2:
                    s_from %= 2
                if sizes[2] == 2:
                    b_from %= 2
                if 0 <= s_from < sizes[1] and 0 <= b_from < sizes[2]:
                    source = ((z ^ exp_bit) * sizes[1] + s_from) * sizes[2] + b_from
                    pairs.append((source, (z * sizes[1] + s) * sizes[2] + b))
    return lax.ppermute(value, ("exp", "strip", "band"), pairs)


def on_device(images, valid_mask, basis_index, match_index, psf_bank):
    count, rows, cols = images.shape
    strips, bands, layers = lax.axis_size("strip"), lax.axis_size("band"), lax.axis_size("exp")
    swap_rows, swap_cols = strips == 2, bands == 2
    f32 = lambda *shape: jax.ShapeDtypeStruct(shape, jnp.float32)
    area = rows * cols

    row_outs = [f32(RIM * count, cols)] * (1 if swap_rows else 2)
    col_outs = [f32(rows, LANES)] * (1 if swap_cols else 2)
    corner_outs = [f32(8, LANES)] * (len(row_outs) * len(col_outs))
    packed = call(
        functools.partial(pack_body, swap_rows, swap_cols), row_outs + col_outs + corner_outs, [VMEM], 100000, 300000
    )(images)
    packed = list(packed)
    ups = [packed.pop(0) for _ in row_outs]
    edges = [packed.pop(0) for _ in col_outs]
    if swap_rows:
        above = below = moved(ups[0], 0, 1, 0)
    else:
        below, above = moved(ups[0], 0, 1, 0), moved(ups[1], 0, -1, 0)
    if swap_cols:
        left = right = moved(edges[0], 0, 0, 1)
    else:
        right, left = moved(edges[0], 0, 0, 1), moved(edges[1], 0, 0, -1)
    corners = {}
    for c in range(len(col_outs)):
        for r in range(len(row_outs)):
            value = packed.pop(0)
            corners[(r, c)] = moved(value, 0, 1 if r == 0 else -1, 1 if c == 0 else -1)
    at = lambda r, c: corners[(0 if swap_rows else r, 0 if swap_cols else c)]
    rims = (above, below, left, right, at(1, 1), at(1, 0), at(0, 1), at(0, 0))

    banks = psf_bank.shape[0]
    taps = call(tap_body, jax.ShapeDtypeStruct((banks, 2 * TILE_ROWS, DEPTH), jnp.bfloat16), [VMEM], 10000000, 300000)(psf_bank)

    def warp(sent):
        return call(
            functools.partial(warp_body, sent),
            f32(count, TILE_ROWS, cols),
            [VMEM, VMEM, SMEM, VMEM] + [VMEM] * 8,
            4 * TILE_ROWS * DEPTH * cols * count * 4,
            1000000,
        )(images, valid_mask, basis_index, taps, *rims)

    sent = moved(warp(True), 1, 0, 0)
    state = call(gather_body, f32(8, TILE_ROWS, cols), [VMEM, VMEM], area * 100, 400000)(warp(False), sent)
    bit = 2
    while bit < layers:
        last = 2 * bit == layers
        out = f32(TILE_ROWS, cols) if last else f32(8, TILE_ROWS, cols)
        state = call(functools.partial(merge_body, last), out, [VMEM, VMEM], area * 20, 300000)(
            state, moved(state, bit, 0, 0)
        )
        bit *= 2
    pair = moved(state, 1, 0, 0)
    if swap_rows:
        same = moved(state, 0, 1, 0)
        cross = moved(state, 1, 1, 0)
        near = (same, cross, same, cross)
    else:
        near = (moved(state, 0, -1, 0), moved(state, 1, -1, 0), moved(state, 0, 1, 0), moved(state, 1, 1, 0))
    side_outs = [f32(rows + 8, LANES)] * (1 if swap_cols else 2)
    coadd, rim, *side = call(
        functools.partial(join_body, swap_cols), [f32(rows, cols), f32(8, cols)] + side_outs, [VMEM] * 6, 10000, 100000
    )(state, pair, *near)
    if swap_cols:
        left = right = moved(side[0], 0, 0, 1)
    else:
        right, left = moved(side[0], 0, 0, 1), moved(side[1], 0, 0, -1)
    difference = call(
        match_body, f32(count, rows, cols), [VMEM, SMEM, VMEM] + [VMEM] * 4, 8 * area * DEPTH * count, 1000000
    )(images, match_index, taps, coadd, rim, left, right)
    return coadd, difference


def solution(mesh):
    return jax.shard_map(
        on_device,
        mesh=mesh,
        in_specs=(
            P(("patch", "exp"), "strip", "band"),
            P(("patch", "exp"), "strip", "band"),
            P(("patch", "exp"), "strip", None),
            P(("patch", "exp"), "strip", None),
            P(),
        ),
        out_specs=(P(("patch", "strip"), "band"), P(("patch", "exp"), "strip", "band")),
        check_vma=False,
    )
```

time: 135 us -> 35.2 us (0.26)
  blocking collectives: 57.3 us -> 0 us
  local copies, waits for them, and re-layouts: 30.3 us -> 3.32 us
  other arithmetic: 21.6 us -> 0 us
  Pallas kernels: 0 us -> 7.27 us
  starting transfers between devices: 17.3 us -> 11.1 us
  waiting for transfers between devices: 6.63 us -> 12.5 us
    all_gather x4 -> x0, blocking collectives: 57.3 us -> none  [joined(): pieces = jax.tree.map(lambda part: lax.all_gather(part, axis), value)]
    slice x33 -> x0, local copies, waits for them, and re-layouts: 26.6 us -> none  [the longest x14 18.6 us: vary_conv(): low_acc = low_acc + kernels[..., 0, tap_at][..., None] * window]
    select_n x2 -> x0, other arithmetic: 11.4 us -> none  [the longest x1 11.3 us: on_device(): jnp.where(is_valid, warped, -sentinel)]
    sub x1 -> x0, other arithmetic: 9.24 us -> none  [on_device(): return (coadd_image, images - matched)]
    pallas_call x0 -> x8, Pallas kernels: none -> 7.27 us  [the longest x2 3.73 us: warp(): call(functools.partial(warp_body, sent), f32(count, TILE_ROWS, cols), [VM...]
    ppermute x8 -> x9, starting transfers between devices: 17.3 us -> 11.1 us  [moved(): return lax.ppermute(value, ('exp', 'strip', 'band'), pairs)]
    ppermute x8 -> x9, waiting for transfers between devices: 6.63 us -> 12.5 us  [moved(): return lax.ppermute(value, ('exp', 'strip', 'band'), pairs)]
    unnamed x19 -> x14, local copies, waits for them, and re-layouts: 3.54 us -> 3.32 us
  transfers between devices with their start and end apart: 8 -> 9, of which waited for: 3 -> 7; matrix products, arithmetic and copies ran while one was open for 18% -> 2% of each run, Pallas kernels for 0% -> 7%
where the time goes in v1:
time: 35.2 us; the launch traced here: 34.8 us
  waiting for transfers between devices  12.5 us (36%)
  starting transfers between devices  11.1 us (32%)
  Pallas kernels  7.27 us (21%)
  local copies, waits for them, and re-layouts  3.32 us (9%)
  between operations  0.7 us (2%)
    ppermute x9, waiting for transfers between devices, moved(): return lax.ppermute(value, ('exp', 'strip', 'band'), pairs)  12.5 us
    ppermute x9, starting transfers between devices, moved(): return lax.ppermute(value, ('exp', 'strip', 'band'), pairs)  11.1 us
    pallas_call x2, Pallas kernels, warp(): call(functools.partial(warp_body, sent), f32(count, TILE_ROWS, cols), [VM...  3.73 us
    unnamed x14, local copies, waits for them, and re-layouts  3.32 us
    pallas_call x1, Pallas kernels, on_device(): call(match_body, f32(count, rows, cols), [VMEM, SMEM, VMEM] + [VMEM] * 4,...  2.08 us
  transfers between devices with their start and end apart: 9, of which 7 were waited for; matrix products, arithmetic and copies ran while one was open for 2% of the time, Pallas kernels for 7%

profile of v1, /device:TPU:0, one launch (start us, length us, event | category | flops | bytes accessed | tf_op | source)
XLA Modules:
  0.0 34.8 jit_solution(11660769036397169453)
XLA Ops:
  0.6 0.9 %copy-done = f32[8,32,256]{2,1,0:T(8,128)S(1)} copy-done((f32[8,32,256]{2,1,0:T(8,128)S(1)}, f32[8,32,256]{2,1,0:T(8,128)}, u32[]{:S(2)}) %copy-start) | copy-done | bytes 262168
  1.6 0.1 shard_map.69
  1.7 3.0 %collective-permute-start = (f32[32,256]{1,0:T(8,128)S(1)}, f32[32,256]{1,0:T(8,128)S(1)}, u32[]{:S(2)}, u32[]{:S(2)}) collective-permute-start(f32[32,256]{1,0:T(8,128)S(1)} %get-tuple-element.8), channel_id=1, source_target_pairs={{2,0},{3,1},{0,2},{1,3},{6,4},{7,5},{4,6},{5,7},{10,8},{11,9},{8,1... | collective-permute-start | bytes 98312 | tf_op jit(solution)/shard_map/ppermute | solution.py:338
  4.8 0.2 collective-permute-start.2
  4.9 0.8 %copy.7.index_ref = s32[8,2,2]{2,1,0:T(2,128)S(1)} copy(s32[8,2,2]{0,2,1:T(2,128)} %param.7) | data formatting | bytes 256 | tf_op args[2]
  5.7 0.7 %copy-done.4 = f32[16,81]{1,0:T(8,128)S(1)} copy-done((f32[16,81]{1,0:T(8,128)S(1)}, f32[16,81]{1,0:T(8,128)}, u32[]{:S(2)}) %copy-start.4) | copy-done | bytes 5208
  6.4 0.5 %shard_map.68.taps_ref = bf16[16,32,256]{2,1,0:T(8,128)(2,1)S(1)} custom-call(f32[16,81]{1,0:T(8,128)S(1)} %copy-done.4), custom_call_target="tpu_custom_call" | custom-call | flops 10000000 | bytes 300000 | tf_op jit(solution)/shard_map/pallas_call | solution.py:374
  6.9 0.8 %collective-permute-done.2.c_al.c_ar.c_bl.c_br = f32[8,128]{1,0:T(8,128)S(1)} collective-permute-done((f32[8,128]{1,0:T(8,128)S(1)}, f32[8,128]{1,0:T(8,128)S(1)}, u32[]{:S(2)}, u32[]{:S(2)}) %collective-permute-start.2) | collective-permute-done | bytes 4128 | tf_op jit(solution)/shard_map/ppermute | solution.py:338
  7.8 1.9 %shard_map.71 = f32[8,16,256]{2,1,0:T(8,128)S(1)} custom-call(f32[8,32,256]{2,1,0:T(8,128)S(1)} %copy-done.1, s32[8,32,256]{2,1,0:T(8,128)S(1)} %copy-done.2, s32[8,2,2]{2,1,0:T(2,128)S(1)} %copy.7.index_ref, bf16[16,32,256]{2,1,0:T(8,128)(2,1)S(1)} %shard_map.68.taps_ref, f32[32,256]{1,0:T(8,128)S(1)} %collective-permute-done.above_ref.below_ref, ...), custom_call_target="tpu_custom_call" | custom-call | flops 134217728 | bytes 1000000 | tf_op jit(solution)/shard_map/pallas_call | solution.py:377
  9.7 1.6 %collective-permute-start.3 = (f32[8,16,256]{2,1,0:T(8,128)S(1)}, f32[8,16,256]{2,1,0:T(8,128)S(1)}, u32[]{:S(2)}, u32[]{:S(2)}) collective-permute-start(f32[8,16,256]{2,1,0:T(8,128)S(1)} %shard_map.71), channel_id=1, source_target_pairs={{4,0},{5,1},{6,2},{7,3},{0,4},{1,5},{2,6},{3,7},{12,8},{13,9},{14,... | collective-permute-start | bytes 393224 | tf_op jit(solution)/shard_map/ppermute | solution.py:338
  11.3 1.9 %shard_map.70.own_ref = f32[8,16,256]{2,1,0:T(8,128)S(1)} custom-call(f32[8,32,256]{2,1,0:T(8,128)S(1)} %copy-done.1, s32[8,32,256]{2,1,0:T(8,128)S(1)} %copy-done.2, s32[8,2,2]{2,1,0:T(2,128)S(1)} %copy.7.index_ref, bf16[16,32,256]{2,1,0:T(8,128)(2,1)S(1)} %shard_map.68.taps_ref, f32[32,256]{1,0:T(8,128)S(1)} %collective-permute-done.above_ref.below_ref, ...), custom_call_target="tpu_custom_call" | custom-call | flops 134217728 | bytes 1000000 | tf_op jit(solution)/shard_map/pallas_call | solution.py:377
  13.2 2.5 %collective-permute-done.3.other_ref = f32[8,16,256]{2,1,0:T(8,128)S(1)} collective-permute-done((f32[8,16,256]{2,1,0:T(8,128)S(1)}, f32[8,16,256]{2,1,0:T(8,128)S(1)}, u32[]{:S(2)}, u32[]{:S(2)}) %collective-permute-start.3) | collective-permute-done | bytes 131104 | tf_op jit(solution)/shard_map/ppermute | solution.py:338
  15.7 0.1 shard_map.72.own_ref
  15.8 2.7 %collective-permute-start.4 = (f32[8,16,256]{2,1,0:T(8,128)S(1)}, f32[8,16,256]{2,1,0:T(8,128)S(1)}, u32[]{:S(2)}, u32[]{:S(2)}) collective-permute-start(f32[8,16,256]{2,1,0:T(8,128)S(1)} %shard_map.72.own_ref), channel_id=1, source_target_pairs={{8,0},{9,1},{10,2},{11,3},{12,4},{13,5},{14,6},{15,7},{0,8},{1,9},... | collective-permute-start | bytes 393224 | tf_op jit(solution)/shard_map/ppermute | solution.py:338
  18.5 6.2 %collective-permute-done.4.other_ref = f32[8,16,256]{2,1,0:T(8,128)S(1)} collective-permute-done((f32[8,16,256]{2,1,0:T(8,128)S(1)}, f32[8,16,256]{2,1,0:T(8,128)S(1)}, u32[]{:S(2)}, u32[]{:S(2)}) %collective-permute-start.4) | collective-permute-done | bytes 131104 | tf_op jit(solution)/shard_map/ppermute | solution.py:338
  24.7 0.7 %collective-permute-start.5 = (f32[16,256]{1,0:T(8,128)S(1)}, f32[16,256]{1,0:T(8,128)S(1)}, u32[]{:S(2)}, u32[]{:S(2)}) collective-permute-start(f32[16,256]{1,0:T(8,128)S(1)} %shard_map.73.own_ref), channel_id=1, source_target_pairs={{4,0},{5,1},{6,2},{7,3},{0,4},{1,5},{2,6},{3,7},{12,8},{13,9},{14,... | collective-permute-start | bytes 49160 | tf_op jit(solution)/shard_map/ppermute | solution.py:338
  25.5 2.7 %collective-permute-start.7 = (f32[16,256]{1,0:T(8,128)S(1)}, f32[16,256]{1,0:T(8,128)S(1)}, u32[]{:S(2)}, u32[]{:S(2)}) collective-permute-start(f32[16,256]{1,0:T(8,128)S(1)} %shard_map.73.own_ref), channel_id=1, source_target_pairs={{6,0},{7,1},{4,2},{5,3},{2,4},{3,5},{0,6},{1,7},{14,8},{15,9},{12,... | collective-permute-start | bytes 49160 | tf_op jit(solution)/shard_map/ppermute | solution.py:338
  28.2 0.2 collective-permute-done.5.pair_ref
  28.5 0.7 %collective-permute-done.6.a_same.b_same = f32[16,256]{1,0:T(8,128)S(1)} collective-permute-done((f32[16,256]{1,0:T(8,128)S(1)}, f32[16,256]{1,0:T(8,128)S(1)}, u32[]{:S(2)}, u32[]{:S(2)}) %collective-permute-start.6) | collective-permute-done | bytes 16416 | tf_op jit(solution)/shard_map/ppermute | solution.py:338
  29.1 1.0 %collective-permute-done.7.a_cross.b_cross = f32[16,256]{1,0:T(8,128)S(1)} collective-permute-done((f32[16,256]{1,0:T(8,128)S(1)}, f32[16,256]{1,0:T(8,128)S(1)}, u32[]{:S(2)}, u32[]{:S(2)}) %collective-permute-start.7) | collective-permute-done | bytes 16416 | tf_op jit(solution)/shard_map/ppermute | solution.py:338
  30.2 0.6 %shard_map.74 = (f32[32,256]{1,0:T(8,128)}, f32[8,256]{1,0:T(8,128)S(1)}, f32[40,128]{1,0:T(8,128)S(1)}) custom-call(f32[16,256]{1,0:T(8,128)S(1)} %shard_map.73.own_ref, f32[16,256]{1,0:T(8,128)S(1)} %collective-permute-done.5.pair_ref, f32[16,256]{1,0:T(8,128)S(1)} %collective-permute-done.6.a_same.b_same, ...), custom_call_target="tpu_custom_call" | custom-call | flops 10000 | bytes 100000 | tf_op jit(solution)/shard_map/pallas_call | solution.py:403
  30.9 1.0 %collective-permute-done.8.left_ref.right_ref = f32[40,128]{1,0:T(8,128)S(1)} collective-permute-done((f32[40,128]{1,0:T(8,128)S(1)}, f32[40,128]{1,0:T(8,128)S(1)}, u32[]{:S(2)}, u32[]{:S(2)}) %collective-permute-start.8) | collective-permute-done | bytes 20512 | tf_op jit(solution)/shard_map/ppermute | solution.py:338
  32.0 0.8 %copy-done.3 = f32[32,256]{1,0:T(8,128)S(1)} copy-done((f32[32,256]{1,0:T(8,128)S(1)}, f32[32,256]{1,0:T(8,128)}, u32[]{:S(2)}) %copy-start.3) | copy-done | bytes 32792
  32.7 2.1 %shard_map.75 = f32[8,32,256]{2,1,0:T(8,128)} custom-call(f32[8,32,256]{2,1,0:T(8,128)S(1)} %copy-done.1, s32[8,2,2]{2,1,0:T(2,128)S(1)} %copy.9.index_ref, bf16[16,32,256]{2,1,0:T(8,128)(2,1)S(1)} %shard_map.68.taps_ref, f32[32,256]{1,0:T(8,128)S(1)} %copy-done.3, f32[8,256]{1,0:T(8,128)S(1)} %get-tuple-element.12.rim_ref, ...), custom_call_target="tpu_custom_call" | custom-call | flops 134217728 | bytes 1000000 | tf_op jit(solution)/shard_map/pallas_call | solution.py:410
  (16 shorter events, 0.3 us)
Async XLA Ops:
  0.6 1.0 %copy-start = (f32[8,32,256]{2,1,0:T(8,128)S(1)}, f32[8,32,256]{2,1,0:T(8,128)}, u32[]{:S(2)}) copy-start(f32[8,32,256]{2,1,0:T(8,128)} %images_ref.7) | copy-start | bytes 786436
  1.6 6.2 %copy-start.1 = (f32[8,32,256]{2,1,0:T(8,128)S(1)}, f32[8,32,256]{2,1,0:T(8,128)}, u32[]{:S(2)}) copy-start(f32[8,32,256]{2,1,0:T(8,128)} %images_ref.7) | copy-start | bytes 786436
  1.6 6.2 %copy-start.2 = (s32[8,32,256]{2,1,0:T(8,128)S(1)}, s32[8,32,256]{2,1,0:T(8,128)}, u32[]{:S(2)}) copy-start(s32[8,32,256]{2,1,0:T(8,128)} %mask_ref.3) | copy-start | bytes 786436
  1.7 6.1 %collective-permute-start = (f32[32,256]{1,0:T(8,128)S(1)}, f32[32,256]{1,0:T(8,128)S(1)}, u32[]{:S(2)}, u32[]{:S(2)}) collective-permute-start(f32[32,256]{1,0:T(8,128)S(1)} %get-tuple-element.8), channel_id=1, source_target_pairs={{2,0},{3,1},{0,2},{1,3},{6,4},{7,5},{4,6},{5,7},{10,8},{11,9},{8,1... | collective-permute-start | bytes 98312 | tf_op jit(solution)/shard_map/ppermute | solution.py:338
  4.8 3.0 %collective-permute-start.1 = (f32[32,128]{1,0:T(8,128)S(1)}, f32[32,128]{1,0:T(8,128)S(1)}, u32[]{:S(2)}, u32[]{:S(2)}) collective-permute-start(f32[32,128]{1,0:T(8,128)S(1)} %get-tuple-element.9), channel_id=1, source_target_pairs={{1,0},{0,1},{3,2},{2,3},{5,4},{4,5},{7,6},{6,7},{9,8},{8,9},{11,10... | collective-permute-start | bytes 49160 | tf_op jit(solution)/shard_map/ppermute | solution.py:338
  4.8 3.0 %collective-permute-start.2 = (f32[8,128]{1,0:T(8,128)S(1)}, f32[8,128]{1,0:T(8,128)S(1)}, u32[]{:S(2)}, u32[]{:S(2)}) collective-permute-start(f32[8,128]{1,0:T(8,128)S(1)} %get-tuple-element.10), channel_id=1, source_target_pairs={{3,0},{2,1},{1,2},{0,3},{7,4},{6,5},{5,6},{4,7},{11,8},{10,9},{9,1... | collective-permute-start | bytes 12296 | tf_op jit(solution)/shard_map/ppermute | solution.py:338
  5.7 0.7 %copy-start.4 = (f32[16,81]{1,0:T(8,128)S(1)}, f32[16,81]{1,0:T(8,128)}, u32[]{:S(2)}) copy-start(f32[16,81]{1,0:T(8,128)} %bank_ref.1) | copy-start | bytes 15556
  9.7 6.0 %collective-permute-start.3 = (f32[8,16,256]{2,1,0:T(8,128)S(1)}, f32[8,16,256]{2,1,0:T(8,128)S(1)}, u32[]{:S(2)}, u32[]{:S(2)}) collective-permute-start(f32[8,16,256]{2,1,0:T(8,128)S(1)} %shard_map.71), channel_id=1, source_target_pairs={{4,0},{5,1},{6,2},{7,3},{0,4},{1,5},{2,6},{3,7},{12,8},{13,9},{14,... | collective-permute-start | bytes 393224 | tf_op jit(solution)/shard_map/ppermute | solution.py:338
  15.8 8.8 %collective-permute-start.4 = (f32[8,16,256]{2,1,0:T(8,128)S(1)}, f32[8,16,256]{2,1,0:T(8,128)S(1)}, u32[]{:S(2)}, u32[]{:S(2)}) collective-permute-start(f32[8,16,256]{2,1,0:T(8,128)S(1)} %shard_map.72.own_ref), channel_id=1, source_target_pairs={{8,0},{9,1},{10,2},{11,3},{12,4},{13,5},{14,6},{15,7},{0,8},{1,9},... | collective-permute-start | bytes 393224 | tf_op jit(solution)/shard_map/ppermute | solution.py:338
  24.7 3.8 %collective-permute-start.5 = (f32[16,256]{1,0:T(8,128)S(1)}, f32[16,256]{1,0:T(8,128)S(1)}, u32[]{:S(2)}, u32[]{:S(2)}) collective-permute-start(f32[16,256]{1,0:T(8,128)S(1)} %shard_map.73.own_ref), channel_id=1, source_target_pairs={{4,0},{5,1},{6,2},{7,3},{0,4},{1,5},{2,6},{3,7},{12,8},{13,9},{14,... | collective-permute-start | bytes 49160 | tf_op jit(solution)/shard_map/ppermute | solution.py:338
  25.4 3.7 %collective-permute-start.6 = (f32[16,256]{1,0:T(8,128)S(1)}, f32[16,256]{1,0:T(8,128)S(1)}, u32[]{:S(2)}, u32[]{:S(2)}) collective-permute-start(f32[16,256]{1,0:T(8,128)S(1)} %shard_map.73.own_ref), channel_id=1, source_target_pairs={{2,0},{3,1},{0,2},{1,3},{6,4},{7,5},{4,6},{5,7},{10,8},{11,9},{8,1... | collective-permute-start | bytes 49160 | tf_op jit(solution)/shard_map/ppermute | solution.py:338
  25.5 4.6 %collective-permute-start.7 = (f32[16,256]{1,0:T(8,128)S(1)}, f32[16,256]{1,0:T(8,128)S(1)}, u32[]{:S(2)}, u32[]{:S(2)}) collective-permute-start(f32[16,256]{1,0:T(8,128)S(1)} %shard_map.73.own_ref), channel_id=1, source_target_pairs={{6,0},{7,1},{4,2},{5,3},{2,4},{3,5},{0,6},{1,7},{14,8},{15,9},{12,... | collective-permute-start | bytes 49160 | tf_op jit(solution)/shard_map/ppermute | solution.py:338
  30.2 0.7 %copy-start.5 = (s32[8,2,2]{0,2,1:T(2,128)S(1)}, s32[8,2,2]{0,2,1:T(2,128)}, u32[]{:S(2)}) copy-start(s32[8,2,2]{0,2,1:T(2,128)} %param.8) | copy-start | bytes 388
  30.8 1.2 %collective-permute-start.8 = (f32[40,128]{1,0:T(8,128)S(1)}, f32[40,128]{1,0:T(8,128)S(1)}, u32[]{:S(2)}, u32[]{:S(2)}) collective-permute-start(f32[40,128]{1,0:T(8,128)S(1)} %get-tuple-element.13), channel_id=1, source_target_pairs={{1,0},{0,1},{3,2},{2,3},{5,4},{4,5},{7,6},{6,7},{9,8},{8,9},{11,10... | collective-permute-start | bytes 61448 | tf_op jit(solution)/shard_map/ppermute | solution.py:338
  32.0 0.8 %copy-start.3 = (f32[32,256]{1,0:T(8,128)S(1)}, f32[32,256]{1,0:T(8,128)}, u32[]{:S(2)}) copy-start(f32[32,256]{1,0:T(8,128)} %get-tuple-element.6.coadd_ref) | copy-start | bytes 98308

commit v2 on v1

--- a/solution.py
+++ b/solution.py
@@ -9,24 +9,27 @@
 
 TILE_ROWS = 16
 KERNEL = 9
+GROUP = 3
 RIM = KERNEL // 2
 SLOTS = TILE_ROWS + 2 * RIM
 LANES = 128
 DEPTH = 256
 SENTINEL = 1.0e30
 LIMIT = 1.0e29
+CHUNKS = 2
 
 VMEM = pl.BlockSpec(memory_space=pltpu.VMEM)
 SMEM = pl.BlockSpec(memory_space=pltpu.SMEM)
 
 
-def call(body, outs, specs, flops, size):
+def call(body, outs, specs, flops, size, scratch=()):
     single = not isinstance(outs, (list, tuple))
     return pl.pallas_call(
         body,
         out_shape=outs,
         in_specs=specs,
         out_specs=VMEM if single else [VMEM] * len(outs),
+        scratch_shapes=scratch,
         compiler_params=pltpu.CompilerParams(vmem_limit_bytes=12 << 20),
         cost_estimate=pl.CostEstimate(flops=flops, bytes_accessed=size, transcendentals=0),
     )
@@ -47,7 +50,7 @@
     return columns.astype(jnp.float32) / float(col_count * lax.axis_size("band") - 1)
 
 
-def tap_body(bank_ref, out_ref):
+def tap_rows(bank_ref):
     bank = bank_ref[...]
     normed = bank / jnp.sum(bank, axis=1, keepdims=True)
     tap = iota((KERNEL * KERNEL, DEPTH), 0)
@@ -60,10 +63,46 @@
     for base in range(bank.shape[0]):
         spread = jnp.broadcast_to(first[base : base + 1], (TILE_ROWS, DEPTH))
         rows = pltpu.roll(spread, 0, 1, stride=1, stride_axis=0)
-        wrapped = jnp.where(slot < SLOTS - RIM, pltpu.roll(rows, DEPTH - RIM, 1), pltpu.roll(rows, SLOTS - RIM, 1))
-        high, low = split(wrapped)
-        out_ref[base, :TILE_ROWS, :] = high
-        out_ref[base, TILE_ROWS:, :] = low
+        yield base, jnp.where(slot < SLOTS - RIM, pltpu.roll(rows, DEPTH - RIM, 1), pltpu.roll(rows, SLOTS - RIM, 1))
+
+
+def match_taps_body(bank_ref, index_ref, _, out_ref, all_ref):
+    tiles, pair, count = index_ref.shape
+    n = 2 * TILE_ROWS
+    for base, rows in tap_rows(bank_ref):
+        high, low = split(rows)
+        all_ref[base, :TILE_ROWS, :] = high
+        all_ref[base, TILE_ROWS:, :] = low
+    for tile in range(tiles):
+        for e in range(count):
+            for k in range(pair):
+                at = n * (2 * e + k)
+                out_ref[tile, at : at + n, :] = all_ref[index_ref[tile, k, e]]
+
+
+def warp_taps_body(bank_ref, index_ref, out_ref, all_ref):
+    tiles, pair, count = index_ref.shape
+    lane = iota((TILE_ROWS, DEPTH), 1)
+    part = GROUP * SLOTS
+    n = GROUP * TILE_ROWS
+    for base, rows in tap_rows(bank_ref):
+        high = rows.astype(jnp.bfloat16).astype(jnp.float32)
+        low = rows - high
+        turned = {(0, 0): high, (1, 0): low}
+
+        def turn(which, steps):
+            if (which, steps) not in turned:
+                turned[which, steps] = pltpu.roll((high, low)[which], (part * steps) % DEPTH, 1)
+            return turned[which, steps]
+
+        for g in range(GROUP):
+            value = jnp.where(lane < part, turn(0, -g), jnp.where(lane < 2 * part, turn(0, 1 - g), turn(1, 2 - g)))
+            value = jnp.where(lane < 3 * part, value, 0.0)
+            all_ref[base, g * TILE_ROWS : (g + 1) * TILE_ROWS, :] = value.astype(jnp.bfloat16)
+    for tile in range(tiles):
+        for e in range(count):
+            for k in range(pair):
+                out_ref[tile, e, k * n : (k + 1) * n, :] = all_ref[index_ref[tile, k, e]]
 
 
 def shifted(rows):
@@ -135,7 +174,7 @@
 
 
 def warp_body(
-    sent, images_ref, mask_ref, index_ref, taps_ref, above_ref, below_ref, left_ref, right_ref, c_al, c_ar, c_bl, c_br, out_ref
+    sent, blocks, images_ref, mask_ref, taps_ref, above_ref, below_ref, left_ref, right_ref, c_al, c_ar, c_bl, c_br, out_ref
 ):
     count, rows, cols = images_ref.shape
     tiles = rows // TILE_ROWS
@@ -147,52 +186,72 @@
     after = pl.multiple_of(jnp.minimum(start + TILE_ROWS, rows - 8), 8)
     top = tile == 0
     end = tile == tiles - 1
-    sub = iota((8, cols), 0)
-    sub_l = iota((8, LANES), 0)
-    lane_l = iota((8, LANES), 1)
-    lane_m = iota((TILE_ROWS, LANES), 1)
+    sub = iota((8, LANES), 0)
+    lane = iota((SLOTS, LANES), 1)
     blend = blend_row(cols)
-
-    def put(first, last, e, lane):
-        first = pltpu.roll(first, (LANES - RIM * e) % LANES, 1) if e else first
-        last = pltpu.roll(last, (LANES - RIM - RIM * e) % LANES, 1)
-        return edge(first, last, right, left, lane)
-
-    rim_first = jnp.where(
-        sub_l < RIM,
-        jnp.where(end, jnp.where(below, c_br[...], 0.0), right_ref[pl.ds(after, 8), :]),
-        jnp.where(top, jnp.where(above, c_ar[...], 0.0), right_ref[pl.ds(prior, 8), :]),
-    )
-    rim_last = jnp.where(
-        sub_l < RIM,
-        jnp.where(end, jnp.where(below, c_bl[...], 0.0), left_ref[pl.ds(after, 8), :]),
-        jnp.where(top, jnp.where(above, c_al[...], 0.0), left_ref[pl.ds(prior, 8), :]),
-    )
-    main_first = right_ref[pl.ds(start, TILE_ROWS), :]
-    main_last = left_ref[pl.ds(start, TILE_ROWS), :]
-    for e in range(count):
-        group = 8 * (e // 2)
-        low_rows = below_ref[group : group + 8, :]
-        high_rows = above_ref[group : group + 8, :]
+    width = 2 * LANES
+
+    def side(ref, corner_above, corner_below):
+        rim = jnp.where(
+            sub < RIM,
+            jnp.where(end, jnp.where(below, corner_below[...], 0.0), ref[pl.ds(after, 8), :]),
+            jnp.where(top, jnp.where(above, corner_above[...], 0.0), ref[pl.ds(prior, 8), :]),
+        )
+        return jnp.concatenate([ref[pl.ds(start, TILE_ROWS), :], rim], axis=0)
+
+    rights = jnp.where(right, side(right_ref, c_ar, c_br), 0.0)
+    lefts = jnp.where(left, side(left_ref, c_al, c_bl), 0.0)
+    last = cols // LANES - 1
+
+    def source(e, block):
+        if block < 0:
+            return pltpu.roll(lefts, (LANES - RIM - RIM * e) % LANES, 1)
+        if block > last:
+            return pltpu.roll(rights, (LANES - RIM * e) % LANES, 1) if e else rights
+        at = slice(block * LANES, (block + 1) * LANES)
+        group = slice(8 * (e // 2), 8 * (e // 2) + 8)
+        low_rows, high_rows = below_ref[group, at], above_ref[group, at]
         if e % 2:
             low_rows = pltpu.roll(low_rows, RIM, 0)
         else:
             high_rows = pltpu.roll(high_rows, RIM, 0)
         rim = jnp.where(
             sub < RIM,
-            jnp.where(end, jnp.where(below, low_rows, 0.0), images_ref[e, pl.ds(after, 8), :]),
-            jnp.where(top, jnp.where(above, high_rows, 0.0), images_ref[e, pl.ds(prior, 8), :]),
+            jnp.where(end, jnp.where(below, low_rows, 0.0), images_ref[e, pl.ds(after, 8), at]),
+            jnp.where(top, jnp.where(above, high_rows, 0.0), images_ref[e, pl.ds(prior, 8), at]),
         )
-        body = jnp.concatenate([images_ref[e, pl.ds(start, TILE_ROWS), :], rim], axis=0)
-        edges = jnp.concatenate([put(main_first, main_last, e, lane_m), put(rim_first, rim_last, e, lane_l)], axis=0)
-        high, low = shifted(jnp.concatenate([body, edges], axis=1))
-        taps = jnp.concatenate([taps_ref[index_ref[e, tile, 0]], taps_ref[index_ref[e, tile, 1]]], axis=0)
-        sums = jnp.dot(taps, high, preferred_element_type=jnp.float32) + jnp.dot(taps, low, preferred_element_type=jnp.float32)
-        n = TILE_ROWS
-        first = sums[0:n] + sums[n : 2 * n]
-        second = sums[2 * n : 3 * n] + sums[3 * n : 4 * n]
-        warped = (1.0 - blend) * first + blend * second
-        out_ref[e] = jnp.where(mask_ref[e, pl.ds(start, TILE_ROWS), :] == 1, warped, SENTINEL)
+        return jnp.concatenate([images_ref[e, pl.ds(start, TILE_ROWS), at], rim], axis=0)
+
+    zero = jnp.zeros((DEPTH - 3 * GROUP * SLOTS, width), jnp.float32)
+    for e in range(count):
+        taps = taps_ref[tile, e]
+        seen = {}
+
+        def get(block):
+            if block not in seen:
+                seen[block] = source(e, block)
+            return seen[block]
+
+        for order, block in enumerate(blocks):
+            rim = jnp.where(lane < RIM, get(block + 1), get(block - 1))
+            field = jnp.concatenate([get(block), rim], axis=1)
+            near = jnp.concatenate([pltpu.roll(field, 1, 1), field, pltpu.roll(field, width - 1, 1)], axis=0)
+            high = near.astype(jnp.bfloat16).astype(jnp.float32)
+            stack = jnp.concatenate([high, near - high, high, zero], axis=0).astype(jnp.bfloat16)
+            sums = jnp.dot(taps, stack, preferred_element_type=jnp.float32)
+            n = TILE_ROWS
+            pair = []
+            for k in range(2):
+                at = k * GROUP * n
+                pair.append(
+                    pltpu.roll(sums[at : at + n], GROUP, 1)[:, :LANES]
+                    + sums[at + n : at + 2 * n, :LANES]
+                    + pltpu.roll(sums[at + 2 * n : at + 3 * n], width - GROUP, 1)[:, :LANES]
+                )
+            here = blend[:, block * LANES : (block + 1) * LANES]
+            warped = (1.0 - here) * pair[0] + here * pair[1]
+            valid = mask_ref[e, pl.ds(start, TILE_ROWS), block * LANES : (block + 1) * LANES] == 1
+            out_ref[e, :, order * LANES : (order + 1) * LANES] = jnp.where(valid, warped, SENTINEL)
 
 
 def insert_low(three, value):
@@ -213,17 +272,17 @@
     return a, b, jnp.maximum(c, less)
 
 
-def gather_body(own_ref, other_ref, out_ref):
-    count, rows, cols = own_ref.shape
+def gather_body(first, own_ref, other_ref, out_ref):
+    count, rows, cols = other_ref.shape
     big = jnp.full((8, LANES), SENTINEL, jnp.float32)
     for r in range(0, rows, 8):
         for c in range(0, cols, LANES):
             total = jnp.zeros((8, LANES), jnp.float32)
             number = jnp.zeros((8, LANES), jnp.float32)
             low, high = (big, big, big), (-big, -big, -big)
-            for ref in (own_ref, other_ref):
+            for ref, at in ((own_ref, c + first), (other_ref, c)):
                 for e in range(count):
-                    value = ref[e, r : r + 8, c : c + LANES]
+                    value = ref[e, r : r + 8, at : at + LANES]
                     valid = value < LIMIT
                     total = total + jnp.where(valid, value, 0.0)
                     number = number + jnp.where(valid, 1.0, 0.0)
@@ -249,22 +308,26 @@
     )
 
 
-def merge_body(last, own_ref, other_ref, out_ref):
-    _, rows, cols = own_ref.shape
-    for r in range(0, rows, 8):
-        for c in range(0, cols, LANES):
-            a = [own_ref[k, r : r + 8, c : c + LANES] for k in range(8)]
-            b = [other_ref[k, r : r + 8, c : c + LANES] for k in range(8)]
-            total, number = a[0] + b[0], a[1] + b[1]
-            low = merge_low(a[2:5], b[2:5])
-            high = merge_high(a[5:8], b[5:8])
-            if last:
-                low_sum = low[0] + low[1] + low[2]
-                high_sum = high[0] + high[1] + high[2]
-                out_ref[r : r + 8, c : c + LANES] = (total - low_sum - high_sum) / (number - 6.0)
-            else:
-                for k, plane in enumerate((total, number) + low + high):
-                    out_ref[k, r : r + 8, c : c + LANES] = plane
+def merge_body(last, _, *refs):
+    *inputs, out_ref = refs
+    for piece in range(len(inputs) // 2):
+        own_ref, other_ref = inputs[2 * piece : 2 * piece + 2]
+        _, rows, cols = own_ref.shape
+        for r in range(0, rows, 8):
+            for c in range(0, cols, LANES):
+                a = [own_ref[k, r : r + 8, c : c + LANES] for k in range(8)]
+                b = [other_ref[k, r : r + 8, c : c + LANES] for k in range(8)]
+                total, number = a[0] + b[0], a[1] + b[1]
+                low = merge_low(a[2:5], b[2:5])
+                high = merge_high(a[5:8], b[5:8])
+                at = piece * cols + c
+                if last:
+                    low_sum = low[0] + low[1] + low[2]
+                    high_sum = high[0] + high[1] + high[2]
+                    out_ref[r : r + 8, at : at + LANES] = (total - low_sum - high_sum) / (number - 6.0)
+                else:
+                    for k, plane in enumerate((total, number) + low + high):
+                        out_ref[k, r : r + 8, at : at + LANES] = plane
 
 
 def join_body(swap_cols, own_ref, pair_ref, a_same, a_cross, b_same, b_cross, coadd_ref, rim_ref, *outs):
@@ -289,9 +352,11 @@
             outs[1][at : at + rows, :] = rights
 
 
-def match_body(images_ref, index_ref, taps_ref, coadd_ref, rim_ref, left_ref, right_ref, out_ref):
+def match_body(images_ref, taps_ref, coadd_ref, rim_ref, left_ref, right_ref, coadd_out, out, out_ref, sems):
     count, rows, cols = images_ref.shape
     tiles = rows // TILE_ROWS
+    whole = pltpu.make_async_copy(coadd_ref, coadd_out, sems.at[tiles])
+    whole.start()
     _, _, left, right = sides()
     blend = blend_row(cols)
     sub = iota((8, cols), 0)
@@ -299,6 +364,7 @@
     sub_l = iota((8, LANES), 0)
     edges = edge(right_ref[...], left_ref[...], right, left, lane)
     n = TILE_ROWS
+    copies = []
     for tile in range(tiles):
         start = tile * n
 
@@ -310,15 +376,18 @@
         body = rims(coadd_ref[...], rim_ref[...], sub)
         side = rims(edges[:rows], edges[rows:], sub_l)
         high, low = shifted(jnp.concatenate([body, side], axis=1))
-        taps = jnp.concatenate([taps_ref[index_ref[e, tile, k]] for e in range(count) for k in range(2)], axis=0)
+        taps = taps_ref[tile]
         sums = jnp.dot(taps, high, preferred_element_type=jnp.float32) + jnp.dot(taps, low, preferred_element_type=jnp.float32)
         for e in range(count):
             at = 4 * n * e
             first = sums[at : at + n] + sums[at + n : at + 2 * n]
             second = sums[at + 2 * n : at + 3 * n] + sums[at + 3 * n : at + 4 * n]
-            out_ref[e, start : start + n, :] = images_ref[e, start : start + n, :] - (
-                (1.0 - blend) * first + blend * second
-            )
+            out_ref[tile, e] = images_ref[e, start : start + n, :] - ((1.0 - blend) * first + blend * second)
+        copies.append(pltpu.make_async_copy(out_ref.at[tile], out.at[:, pl.ds(start, n), :], sems.at[tile]))
+        copies[-1].start()
+    for copy in copies:
+        copy.wait()
+    whole.wait()
 
 
 def moved(value, exp_bit, strip_step, band_step):
@@ -371,27 +440,62 @@
     rims = (above, below, left, right, at(1, 1), at(1, 0), at(0, 1), at(0, 0))
 
     banks = psf_bank.shape[0]
-    taps = call(tap_body, jax.ShapeDtypeStruct((banks, 2 * TILE_ROWS, DEPTH), jnp.bfloat16), [VMEM], 10000000, 300000)(psf_bank)
-
-    def warp(sent):
+    tiles = rows // TILE_ROWS
+    turned = lambda index: jnp.transpose(index, (1, 2, 0))
+    scratch = lambda n: [pltpu.VMEM((banks, n, DEPTH), jnp.bfloat16)]
+    half = jnp.bfloat16
+    warp_taps = call(
+        warp_taps_body,
+        jax.ShapeDtypeStruct((tiles, count, 2 * GROUP * TILE_ROWS, DEPTH), half),
+        [VMEM, SMEM],
+        10000000,
+        300000,
+        scratch(GROUP * TILE_ROWS),
+    )(psf_bank, turned(basis_index))
+
+    blocks = list(range(cols // LANES))
+    pieces = [blocks] if CHUNKS == 1 else [[b] for b in blocks]
+
+    def warp(sent, piece):
         return call(
-            functools.partial(warp_body, sent),
-            f32(count, TILE_ROWS, cols),
-            [VMEM, VMEM, SMEM, VMEM] + [VMEM] * 8,
-            4 * TILE_ROWS * DEPTH * cols * count * 4,
+            functools.partial(warp_body, sent, piece),
+            f32(count, TILE_ROWS, LANES * len(piece)),
+            [VMEM, VMEM, VMEM] + [VMEM] * 8,
+            2 * TILE_ROWS * DEPTH * LANES * len(piece) * count * 12,
             1000000,
-        )(images, valid_mask, basis_index, taps, *rims)
-
-    sent = moved(warp(True), 1, 0, 0)
-    state = call(gather_body, f32(8, TILE_ROWS, cols), [VMEM, VMEM], area * 100, 400000)(warp(False), sent)
+        )(images, valid_mask, warp_taps, *rims)
+
+    sents = [moved(warp(True, piece), 1, 0, 0) for piece in pieces]
+    own = warp(False, blocks)
+    states = [
+        call(functools.partial(gather_body, LANES * piece[0]), f32(8, *sent.shape[1:]), [VMEM, VMEM], area * 100, 400000)(
+            own, sent
+        )
+        for piece, sent in zip(pieces, sents)
+    ]
+    match_taps = call(
+        match_taps_body,
+        jax.ShapeDtypeStruct((tiles, 4 * TILE_ROWS * count, DEPTH), half),
+        [VMEM, SMEM, pl.BlockSpec(memory_space=pl.ANY)],
+        10000000,
+        300000,
+        scratch(2 * TILE_ROWS),
+    )(psf_bank, turned(match_index), states[0])
     bit = 2
     while bit < layers:
-        last = 2 * bit == layers
-        out = f32(TILE_ROWS, cols) if last else f32(8, TILE_ROWS, cols)
-        state = call(functools.partial(merge_body, last), out, [VMEM, VMEM], area * 20, 300000)(
-            state, moved(state, bit, 0, 0)
-        )
+        others = [moved(state, bit, 0, 0) for state in states]
+        if 2 * bit == layers:
+            groups = [[x for both in zip(states, others) for x in both]]
+            outs = [f32(TILE_ROWS, cols)]
+        else:
+            groups = [list(both) for both in zip(states, others)]
+            outs = [f32(*state.shape) for state in states]
+        states = [
+            call(functools.partial(merge_body, 2 * bit == layers), out, [pl.BlockSpec(memory_space=pl.ANY)] + [VMEM] * len(group), area * 20, 300000)(match_taps, *group)
+            for out, group in zip(outs, groups)
+        ]
         bit *= 2
+    (state,) = states
     pair = moved(state, 1, 0, 0)
     if swap_rows:
         same = moved(state, 0, 1, 0)
@@ -407,10 +511,15 @@
         left = right = moved(side[0], 0, 0, 1)
     else:
         right, left = moved(side[0], 0, 0, 1), moved(side[1], 0, 0, -1)
-    difference = call(
-        match_body, f32(count, rows, cols), [VMEM, SMEM, VMEM] + [VMEM] * 4, 8 * area * DEPTH * count, 1000000
-    )(images, match_index, taps, coadd, rim, left, right)
-    return coadd, difference
+    return pl.pallas_call(
+        match_body,
+        out_shape=[f32(rows, cols), f32(count, rows, cols)],
+        in_specs=[VMEM] * 6,
+        out_specs=[pl.BlockSpec(memory_space=pl.ANY)] * 2,
+        scratch_shapes=[pltpu.VMEM((tiles, count, TILE_ROWS, cols), jnp.float32), pltpu.SemaphoreType.DMA((tiles + 1,))],
+        compiler_params=pltpu.CompilerParams(vmem_limit_bytes=12 << 20),
+        cost_estimate=pl.CostEstimate(flops=8 * area * DEPTH * count, bytes_accessed=1000000, transcendentals=0),
+    )(images, match_taps, coadd, rim, left, right)
 
 
 def solution(mesh):

time: 35.2 us -> 31.2 us (0.89)
  waiting for transfers between devices: 12.5 us -> 9.28 us
  starting transfers between devices: 11.1 us -> 13.5 us
  local copies, waits for them, and re-layouts: 3.32 us -> 1.43 us
  Pallas kernels: 7.27 us -> 6.08 us
    ppermute x9 -> x11, waiting for transfers between devices: 12.5 us -> 9.28 us  [moved(): return lax.ppermute(value, ('exp', 'strip', 'band'), pairs)]
    ppermute x9 -> x11, starting transfers between devices: 11.1 us -> 13.5 us  [moved(): return lax.ppermute(value, ('exp', 'strip', 'band'), pairs)]
    unnamed x14 -> x12, local copies, waits for them, and re-layouts: 3.32 us -> 1.43 us
    pallas_call x1, Pallas kernels: 0.62 us -> 0.01 us  [on_device(): call(functools.partial(join_body, swap_cols), [f32(rows, cols), f32(8, co...]
    pallas_call x6 -> x9, Pallas kernels: 6.52 us -> 5.94 us  [the longest x3 1.87 us: warp(): call(functools.partial(warp_body, sent, piece), f32(count, TILE_ROWS, LAN...]
  transfers between devices with their start and end apart: 9 -> 11, of which waited for: 7 -> 7; matrix products, arithmetic and copies ran while one was open for 2% -> 0% of each run, Pallas kernels for 7% -> 13%
where the time goes in v2:
time: 31.2 us; the launch traced here: 31.1 us
  starting transfers between devices  13.5 us (43%)
  waiting for transfers between devices  9.28 us (30%)
  Pallas kernels  6.08 us (19%)
  local copies, waits for them, and re-layouts  1.43 us (5%)
  between operations  0.74 us (2%)
    ppermute x11, starting transfers between devices, moved(): return lax.ppermute(value, ('exp', 'strip', 'band'), pairs)  13.5 us
    ppermute x11, waiting for transfers between devices, moved(): return lax.ppermute(value, ('exp', 'strip', 'band'), pairs)  9.28 us
    pallas_call x3, Pallas kernels, warp(): call(functools.partial(warp_body, sent, piece), f32(count, TILE_ROWS, LAN...  1.87 us
    pallas_call x1, Pallas kernels, on_device(): pl.pallas_call(match_body, out_shape=[f32(rows, cols), f32(count, rows, c...  1.44 us
    unnamed x12, local copies, waits for them, and re-layouts  1.43 us
    pallas_call x1, Pallas kernels, on_device(): call(warp_taps_body, jax.ShapeDtypeStruct((tiles, count, 2 * GROUP * TILE...  1.32 us
    pallas_call x1, Pallas kernels, on_device(): call(match_taps_body, jax.ShapeDtypeStruct((tiles, 4 * TILE_ROWS * count,...  1.13 us
  transfers between devices with their start and end apart: 11, of which 7 were waited for; matrix products, arithmetic and copies ran while one was open for 0% of the time, Pallas kernels for 13%

profile of v2, /device:TPU:0, one launch (start us, length us, event | category | flops | bytes accessed | tf_op | source)
XLA Modules:
  0.0 31.1 jit_solution(6969373232053099070)
XLA Ops:
  0.6 0.9 %copy-done = f32[8,32,256]{2,1,0:T(8,128)S(1)} copy-done((f32[8,32,256]{2,1,0:T(8,128)S(1)}, f32[8,32,256]{2,1,0:T(8,128)}, u32[]{:S(2)}) %copy-start) | copy-done | bytes 262168
  1.7 3.0 %collective-permute-start = (f32[32,256]{1,0:T(8,128)S(1)}, f32[32,256]{1,0:T(8,128)S(1)}, u32[]{:S(2)}, u32[]{:S(2)}) collective-permute-start(f32[32,256]{1,0:T(8,128)S(1)} %get-tuple-element.8), channel_id=1, source_target_pairs={{2,0},{3,1},{0,2},{1,3},{6,4},{7,5},{4,6},{5,7},{10,8},{11,9},{8,1... | collective-permute-start | bytes 98312 | tf_op jit(solution)/shard_map/ppermute | solution.py:407
  4.8 0.2 collective-permute-start.2
  5.0 0.5 %copy-done.4 = s32[8,2,2]{0,2,1:T(2,128)S(1)} copy-done((s32[8,2,2]{0,2,1:T(2,128)S(1)}, s32[8,2,2]{0,2,1:T(2,128)}, u32[]{:S(2)}) %copy-start.4) | copy-done | bytes 152
  5.4 1.3 %shard_map.68.taps_ref = bf16[2,8,96,256]{3,2,1,0:T(8,128)(2,1)S(1)} custom-call(f32[16,81]{1,0:T(8,128)S(1)} %copy-done.3, s32[2,2,8]{2,1,0:T(2,128)S(1)} %bitcast.2), custom_call_target="tpu_custom_call" | custom-call | flops 10000000 | bytes 300000 | tf_op jit(solution)/shard_map/pallas_call | solution.py:447
  6.8 1.0 %collective-permute-done.2.c_al.c_ar.c_bl.c_br = f32[8,128]{1,0:T(8,128)S(1)} collective-permute-done((f32[8,128]{1,0:T(8,128)S(1)}, f32[8,128]{1,0:T(8,128)S(1)}, u32[]{:S(2)}, u32[]{:S(2)}) %collective-permute-start.2) | collective-permute-done | bytes 4128 | tf_op jit(solution)/shard_map/ppermute | solution.py:407
  7.8 0.6 %shard_map.71 = f32[8,16,128]{2,1,0:T(8,128)S(1)} custom-call(f32[8,32,256]{2,1,0:T(8,128)S(1)} %copy-done.1, s32[8,32,256]{2,1,0:T(8,128)S(1)} %copy-done.2, bf16[2,8,96,256]{3,2,1,0:T(8,128)(2,1)S(1)} %shard_map.68.taps_ref, f32[32,256]{1,0:T(8,128)S(1)} %collective-permute-done.above_ref.below_ref, ...), custom_call_target="tpu_custom_call" | custom-call | flops 100663296 | bytes 1000000 | tf_op jit(solution)/shard_map/pallas_call | solution.py:460
  8.4 1.6 %collective-permute-start.3 = (f32[8,16,128]{2,1,0:T(8,128)S(1)}, f32[8,16,128]{2,1,0:T(8,128)S(1)}, u32[]{:S(2)}, u32[]{:S(2)}) collective-permute-start(f32[8,16,128]{2,1,0:T(8,128)S(1)} %shard_map.71), channel_id=1, source_target_pairs={{4,0},{5,1},{6,2},{7,3},{0,4},{1,5},{2,6},{3,7},{12,8},{13,9},{14,... | collective-permute-start | bytes 196616 | tf_op jit(solution)/shard_map/ppermute | solution.py:407
  10.0 0.6 %shard_map.74 = f32[8,16,128]{2,1,0:T(8,128)S(1)} custom-call(f32[8,32,256]{2,1,0:T(8,128)S(1)} %copy-done.1, s32[8,32,256]{2,1,0:T(8,128)S(1)} %copy-done.2, bf16[2,8,96,256]{3,2,1,0:T(8,128)(2,1)S(1)} %shard_map.68.taps_ref, f32[32,256]{1,0:T(8,128)S(1)} %collective-permute-done.above_ref.below_ref, ...), custom_call_target="tpu_custom_call" | custom-call | flops 100663296 | bytes 1000000 | tf_op jit(solution)/shard_map/pallas_call | solution.py:460
  10.6 0.5 %collective-permute-start.5 = (f32[8,16,128]{2,1,0:T(8,128)S(1)}, f32[8,16,128]{2,1,0:T(8,128)S(1)}, u32[]{:S(2)}, u32[]{:S(2)}) collective-permute-start(f32[8,16,128]{2,1,0:T(8,128)S(1)} %shard_map.74), channel_id=1, source_target_pairs={{4,0},{5,1},{6,2},{7,3},{0,4},{1,5},{2,6},{3,7},{12,8},{13,9},{14,... | collective-permute-start | bytes 196616 | tf_op jit(solution)/shard_map/ppermute | solution.py:407
  11.1 0.7 %shard_map.70.own_ref = f32[8,16,256]{2,1,0:T(8,128)S(1)} custom-call(f32[8,32,256]{2,1,0:T(8,128)S(1)} %copy-done.1, s32[8,32,256]{2,1,0:T(8,128)S(1)} %copy-done.2, bf16[2,8,96,256]{3,2,1,0:T(8,128)(2,1)S(1)} %shard_map.68.taps_ref, f32[32,256]{1,0:T(8,128)S(1)} %collective-permute-done.above_ref.below_ref, ...), custom_call_target="tpu_custom_call" | custom-call | flops 201326592 | bytes 1000000 | tf_op jit(solution)/shard_map/pallas_call | solution.py:460
  11.9 1.1 %collective-permute-done.3.other_ref = f32[8,16,128]{2,1,0:T(8,128)S(1)} collective-permute-done((f32[8,16,128]{2,1,0:T(8,128)S(1)}, f32[8,16,128]{2,1,0:T(8,128)S(1)}, u32[]{:S(2)}, u32[]{:S(2)}) %collective-permute-start.3) | collective-permute-done | bytes 65568 | tf_op jit(solution)/shard_map/ppermute | solution.py:407
  13.1 2.7 %collective-permute-start.4 = (f32[8,16,128]{2,1,0:T(8,128)S(1)}, f32[8,16,128]{2,1,0:T(8,128)S(1)}, u32[]{:S(2)}, u32[]{:S(2)}) collective-permute-start(f32[8,16,128]{2,1,0:T(8,128)S(1)} %shard_map.72._.refs_0_), channel_id=1, source_target_pairs={{8,0},{9,1},{10,2},{11,3},{12,4},{13,5},{14,6},{15,7},{0,8},{1,9},... | collective-permute-start | bytes 196616 | tf_op jit(solution)/shard_map/ppermute | solution.py:407
  15.8 1.9 %collective-permute-start.6 = (f32[8,16,128]{2,1,0:T(8,128)S(1)}, f32[8,16,128]{2,1,0:T(8,128)S(1)}, u32[]{:S(2)}, u32[]{:S(2)}) collective-permute-start(f32[8,16,128]{2,1,0:T(8,128)S(1)} %shard_map.75.refs_2_), channel_id=1, source_target_pairs={{8,0},{9,1},{10,2},{11,3},{12,4},{13,5},{14,6},{15,7},{0,8},{1,9},... | collective-permute-start | bytes 196616 | tf_op jit(solution)/shard_map/ppermute | solution.py:407
  17.7 1.1 %shard_map.73._.taps_ref = bf16[2,512,256]{2,1,0:T(8,128)(2,1)S(1)} custom-call(f32[16,81]{1,0:T(8,128)S(1)} %copy-done.3, s32[2,2,8]{2,1,0:T(2,128)S(1)} %bitcast.3, f32[8,16,128]{2,1,0:T(8,128)S(1)} %shard_map.72._.refs_0_), custom_call_target="tpu_custom_call" | custom-call | flops 10000000 | bytes 300000 | tf_op jit(solution)/shard_map/pallas_call | solution.py:476
  18.8 2.7 %collective-permute-done.6.refs_3_ = f32[8,16,128]{2,1,0:T(8,128)S(1)} collective-permute-done((f32[8,16,128]{2,1,0:T(8,128)S(1)}, f32[8,16,128]{2,1,0:T(8,128)S(1)}, u32[]{:S(2)}, u32[]{:S(2)}) %collective-permute-start.6) | collective-permute-done | bytes 65568 | tf_op jit(solution)/shard_map/ppermute | solution.py:407
  21.6 1.9 %collective-permute-start.9 = (f32[16,256]{1,0:T(8,128)S(1)}, f32[16,256]{1,0:T(8,128)S(1)}, u32[]{:S(2)}, u32[]{:S(2)}) collective-permute-start(f32[16,256]{1,0:T(8,128)S(1)} %shard_map.76.own_ref), channel_id=1, source_target_pairs={{6,0},{7,1},{4,2},{5,3},{2,4},{3,5},{0,6},{1,7},{14,8},{15,9},{12,... | collective-permute-start | bytes 49160 | tf_op jit(solution)/shard_map/ppermute | solution.py:407
  23.4 1.2 %collective-permute-start.8 = (f32[16,256]{1,0:T(8,128)S(1)}, f32[16,256]{1,0:T(8,128)S(1)}, u32[]{:S(2)}, u32[]{:S(2)}) collective-permute-start(f32[16,256]{1,0:T(8,128)S(1)} %shard_map.76.own_ref), channel_id=1, source_target_pairs={{2,0},{3,1},{0,2},{1,3},{6,4},{7,5},{4,6},{5,7},{10,8},{11,9},{8,1... | collective-permute-start | bytes 49160 | tf_op jit(solution)/shard_map/ppermute | solution.py:407
  24.6 0.5 %collective-permute-start.7 = (f32[16,256]{1,0:T(8,128)S(1)}, f32[16,256]{1,0:T(8,128)S(1)}, u32[]{:S(2)}, u32[]{:S(2)}) collective-permute-start(f32[16,256]{1,0:T(8,128)S(1)} %shard_map.76.own_ref), channel_id=1, source_target_pairs={{4,0},{5,1},{6,2},{7,3},{0,4},{1,5},{2,6},{3,7},{12,8},{13,9},{14,... | collective-permute-start | bytes 49160 | tf_op jit(solution)/shard_map/ppermute | solution.py:407
  25.1 1.1 %collective-permute-done.9.a_cross.b_cross = f32[16,256]{1,0:T(8,128)S(1)} collective-permute-done((f32[16,256]{1,0:T(8,128)S(1)}, f32[16,256]{1,0:T(8,128)S(1)}, u32[]{:S(2)}, u32[]{:S(2)}) %collective-permute-start.9) | collective-permute-done | bytes 16416 | tf_op jit(solution)/shard_map/ppermute | solution.py:407
  26.3 0.9 %collective-permute-done.8.a_same.b_same = f32[16,256]{1,0:T(8,128)S(1)} collective-permute-done((f32[16,256]{1,0:T(8,128)S(1)}, f32[16,256]{1,0:T(8,128)S(1)}, u32[]{:S(2)}, u32[]{:S(2)}) %collective-permute-start.8) | collective-permute-done | bytes 16416 | tf_op jit(solution)/shard_map/ppermute | solution.py:407
  27.2 1.2 %collective-permute-done.7.pair_ref = f32[16,256]{1,0:T(8,128)S(1)} collective-permute-done((f32[16,256]{1,0:T(8,128)S(1)}, f32[16,256]{1,0:T(8,128)S(1)}, u32[]{:S(2)}, u32[]{:S(2)}) %collective-permute-start.7) | collective-permute-done | bytes 16416 | tf_op jit(solution)/shard_map/ppermute | solution.py:407
  28.5 1.2 %collective-permute-done.10.left_ref.right_ref = f32[40,128]{1,0:T(8,128)S(1)} collective-permute-done((f32[40,128]{1,0:T(8,128)S(1)}, f32[40,128]{1,0:T(8,128)S(1)}, u32[]{:S(2)}, u32[]{:S(2)}) %collective-permute-start.10) | collective-permute-done | bytes 20512 | tf_op jit(solution)/shard_map/ppermute | solution.py:407
  29.6 1.4 %shard_map.78 = (f32[32,256]{1,0:T(8,128)}, f32[8,32,256]{2,1,0:T(8,128)}) custom-call(f32[8,32,256]{2,1,0:T(8,128)S(1)} %copy-done.1, bf16[2,512,256]{2,1,0:T(8,128)(2,1)S(1)} %shard_map.73._.taps_ref, f32[32,256]{1,0:T(8,128)S(1)} %get-tuple-element.11.coadd_ref, f32[8,256]{1,0:T(8,128)S(1)} %get-tuple-element.12.rim_ref, ...), custom_call_target="tpu_custom_call" | custom-call | flops 134217728 | bytes 1000000 | tf_op jit(solution)/shard_map/pallas_call | solution.py:514
  (21 shorter events, 0.4 us)
Async XLA Ops:
  0.6 1.0 %copy-start = (f32[8,32,256]{2,1,0:T(8,128)S(1)}, f32[8,32,256]{2,1,0:T(8,128)}, u32[]{:S(2)}) copy-start(f32[8,32,256]{2,1,0:T(8,128)} %images_ref.9) | copy-start | bytes 786436
  1.6 3.4 %copy-start.3 = (f32[16,81]{1,0:T(8,128)S(1)}, f32[16,81]{1,0:T(8,128)}, u32[]{:S(2)}) copy-start(f32[16,81]{1,0:T(8,128)} %bank_ref.3) | copy-start | bytes 15556
  1.7 6.1 %collective-permute-start = (f32[32,256]{1,0:T(8,128)S(1)}, f32[32,256]{1,0:T(8,128)S(1)}, u32[]{:S(2)}, u32[]{:S(2)}) collective-permute-start(f32[32,256]{1,0:T(8,128)S(1)} %get-tuple-element.8), channel_id=1, source_target_pairs={{2,0},{3,1},{0,2},{1,3},{6,4},{7,5},{4,6},{5,7},{10,8},{11,9},{8,1... | collective-permute-start | bytes 98312 | tf_op jit(solution)/shard_map/ppermute | solution.py:407
  4.8 0.7 %copy-start.4 = (s32[8,2,2]{0,2,1:T(2,128)S(1)}, s32[8,2,2]{0,2,1:T(2,128)}, u32[]{:S(2)}) copy-start(s32[8,2,2]{0,2,1:T(2,128)} %param.7) | copy-start | bytes 388
  4.8 3.0 %collective-permute-start.1 = (f32[32,128]{1,0:T(8,128)S(1)}, f32[32,128]{1,0:T(8,128)S(1)}, u32[]{:S(2)}, u32[]{:S(2)}) collective-permute-start(f32[32,128]{1,0:T(8,128)S(1)} %get-tuple-element.9), channel_id=1, source_target_pairs={{1,0},{0,1},{3,2},{2,3},{5,4},{4,5},{7,6},{6,7},{9,8},{8,9},{11,10... | collective-permute-start | bytes 49160 | tf_op jit(solution)/shard_map/ppermute | solution.py:407
  4.8 3.0 %collective-permute-start.2 = (f32[8,128]{1,0:T(8,128)S(1)}, f32[8,128]{1,0:T(8,128)S(1)}, u32[]{:S(2)}, u32[]{:S(2)}) collective-permute-start(f32[8,128]{1,0:T(8,128)S(1)} %get-tuple-element.10), channel_id=1, source_target_pairs={{3,0},{2,1},{1,2},{0,3},{7,4},{6,5},{5,6},{4,7},{11,8},{10,9},{9,1... | collective-permute-start | bytes 12296 | tf_op jit(solution)/shard_map/ppermute | solution.py:407
  5.4 2.4 %copy-start.1 = (f32[8,32,256]{2,1,0:T(8,128)S(1)}, f32[8,32,256]{2,1,0:T(8,128)}, u32[]{:S(2)}) copy-start(f32[8,32,256]{2,1,0:T(8,128)} %images_ref.9) | copy-start | bytes 786436
  5.4 2.4 %copy-start.2 = (s32[8,32,256]{2,1,0:T(8,128)S(1)}, s32[8,32,256]{2,1,0:T(8,128)}, u32[]{:S(2)}) copy-start(s32[8,32,256]{2,1,0:T(8,128)} %mask_ref.5) | copy-start | bytes 786436
  8.4 4.6 %collective-permute-start.3 = (f32[8,16,128]{2,1,0:T(8,128)S(1)}, f32[8,16,128]{2,1,0:T(8,128)S(1)}, u32[]{:S(2)}, u32[]{:S(2)}) collective-permute-start(f32[8,16,128]{2,1,0:T(8,128)S(1)} %shard_map.71), channel_id=1, source_target_pairs={{4,0},{5,1},{6,2},{7,3},{0,4},{1,5},{2,6},{3,7},{12,8},{13,9},{14,... | collective-permute-start | bytes 196616 | tf_op jit(solution)/shard_map/ppermute | solution.py:407
  10.6 5.1 %collective-permute-start.5 = (f32[8,16,128]{2,1,0:T(8,128)S(1)}, f32[8,16,128]{2,1,0:T(8,128)S(1)}, u32[]{:S(2)}, u32[]{:S(2)}) collective-permute-start(f32[8,16,128]{2,1,0:T(8,128)S(1)} %shard_map.74), channel_id=1, source_target_pairs={{4,0},{5,1},{6,2},{7,3},{0,4},{1,5},{2,6},{3,7},{12,8},{13,9},{14,... | collective-permute-start | bytes 196616 | tf_op jit(solution)/shard_map/ppermute | solution.py:407
  13.1 5.8 %collective-permute-start.4 = (f32[8,16,128]{2,1,0:T(8,128)S(1)}, f32[8,16,128]{2,1,0:T(8,128)S(1)}, u32[]{:S(2)}, u32[]{:S(2)}) collective-permute-start(f32[8,16,128]{2,1,0:T(8,128)S(1)} %shard_map.72._.refs_0_), channel_id=1, source_target_pairs={{8,0},{9,1},{10,2},{11,3},{12,4},{13,5},{14,6},{15,7},{0,8},{1,9},... | collective-permute-start | bytes 196616 | tf_op jit(solution)/shard_map/ppermute | solution.py:407
  15.7 2.0 %copy-start.5 = (s32[8,2,2]{0,2,1:T(2,128)S(1)}, s32[8,2,2]{0,2,1:T(2,128)}, u32[]{:S(2)}) copy-start(s32[8,2,2]{0,2,1:T(2,128)} %param.8) | copy-start | bytes 388
  15.8 5.7 %collective-permute-start.6 = (f32[8,16,128]{2,1,0:T(8,128)S(1)}, f32[8,16,128]{2,1,0:T(8,128)S(1)}, u32[]{:S(2)}, u32[]{:S(2)}) collective-permute-start(f32[8,16,128]{2,1,0:T(8,128)S(1)} %shard_map.75.refs_2_), channel_id=1, source_target_pairs={{8,0},{9,1},{10,2},{11,3},{12,4},{13,5},{14,6},{15,7},{0,8},{1,9},... | collective-permute-start | bytes 196616 | tf_op jit(solution)/shard_map/ppermute | solution.py:407
  21.6 4.7 %collective-permute-start.9 = (f32[16,256]{1,0:T(8,128)S(1)}, f32[16,256]{1,0:T(8,128)S(1)}, u32[]{:S(2)}, u32[]{:S(2)}) collective-permute-start(f32[16,256]{1,0:T(8,128)S(1)} %shard_map.76.own_ref), channel_id=1, source_target_pairs={{6,0},{7,1},{4,2},{5,3},{2,4},{3,5},{0,6},{1,7},{14,8},{15,9},{12,... | collective-permute-start | bytes 49160 | tf_op jit(solution)/shard_map/ppermute | solution.py:407
  23.4 3.7 %collective-permute-start.8 = (f32[16,256]{1,0:T(8,128)S(1)}, f32[16,256]{1,0:T(8,128)S(1)}, u32[]{:S(2)}, u32[]{:S(2)}) collective-permute-start(f32[16,256]{1,0:T(8,128)S(1)} %shard_map.76.own_ref), channel_id=1, source_target_pairs={{2,0},{3,1},{0,2},{1,3},{6,4},{7,5},{4,6},{5,7},{10,8},{11,9},{8,1... | collective-permute-start | bytes 49160 | tf_op jit(solution)/shard_map/ppermute | solution.py:407
  24.6 3.7 %collective-permute-start.7 = (f32[16,256]{1,0:T(8,128)S(1)}, f32[16,256]{1,0:T(8,128)S(1)}, u32[]{:S(2)}, u32[]{:S(2)}) collective-permute-start(f32[16,256]{1,0:T(8,128)S(1)} %shard_map.76.own_ref), channel_id=1, source_target_pairs={{4,0},{5,1},{6,2},{7,3},{0,4},{1,5},{2,6},{3,7},{12,8},{13,9},{14,... | collective-permute-start | bytes 49160 | tf_op jit(solution)/shard_map/ppermute | solution.py:407
  28.4 1.3 %collective-permute-start.10 = (f32[40,128]{1,0:T(8,128)S(1)}, f32[40,128]{1,0:T(8,128)S(1)}, u32[]{:S(2)}, u32[]{:S(2)}) collective-permute-start(f32[40,128]{1,0:T(8,128)S(1)} %get-tuple-element.13), channel_id=1, source_target_pairs={{1,0},{0,1},{3,2},{2,3},{5,4},{4,5},{7,6},{6,7},{9,8},{8,9},{11,10... | collective-permute-start | bytes 61448 | tf_op jit(solution)/shard_map/ppermute | solution.py:407

commit v3 on v2

--- a/solution.py
+++ b/solution.py
@@ -272,7 +272,12 @@
     return a, b, jnp.maximum(c, less)
 
 
-def gather_body(first, own_ref, other_ref, out_ref):
+def odd_tile():
+    return (lax.axis_index("exp") + lax.axis_index("strip")) % 2 == 1
+
+
+def gather_body(first, edges, own_ref, other_ref, *refs):
+    out_ref = refs[-2] if edges else refs[-1]
     count, rows, cols = other_ref.shape
     big = jnp.full((8, LANES), SENTINEL, jnp.float32)
     for r in range(0, rows, 8):
@@ -290,6 +295,23 @@
                     high = insert_high(high, jnp.where(valid, value, -SENTINEL))
             for k, plane in enumerate((total, number) + low + high):
                 out_ref[k, r : r + 8, c : c + LANES] = plane
+    if edges:
+        edge_rows(list(refs[:-2]) + [out_ref], refs[-1])
+
+
+def edge_rows(states, edge_ref):
+    odd = odd_tile()
+    at = 0
+    for ref in states:
+        planes, rows, cols = ref.shape
+        sub = iota((8, cols), 0)
+        for p in range(planes // 2):
+            head = [ref[2 * p + k, 0:8, :] for k in range(2)]
+            tail = [ref[2 * p + k, rows - 8 : rows, :] for k in range(2)]
+            even_value = jnp.where(sub < RIM, head[0], pltpu.roll(head[1], RIM, 0))
+            odd_value = jnp.where(sub < RIM, pltpu.roll(tail[0], RIM, 0), tail[1])
+            edge_ref[8 * p : 8 * p + 8, at : at + cols] = jnp.where(odd, odd_value, even_value)
+        at += cols
 
 
 def merge_low(a, b):
@@ -308,40 +330,59 @@
     )
 
 
-def merge_body(last, _, *refs):
+def finish(a, b):
+    total, number = a[0] + b[0], a[1] + b[1]
+    low = merge_low(a[2:5], b[2:5])
+    high = merge_high(a[5:8], b[5:8])
+    low_sum = low[0] + low[1] + low[2]
+    high_sum = high[0] + high[1] + high[2]
+    return (total - low_sum - high_sum) / (number - 6.0)
+
+
+def merge_body(edges, own_ref, other_ref, *refs):
+    out_ref = refs[-2] if edges else refs[-1]
+    _, rows, cols = own_ref.shape
+    for r in range(0, rows, 8):
+        for c in range(0, cols, LANES):
+            a = [own_ref[k, r : r + 8, c : c + LANES] for k in range(8)]
+            b = [other_ref[k, r : r + 8, c : c + LANES] for k in range(8)]
+            planes = (a[0] + b[0], a[1] + b[1]) + merge_low(a[2:5], b[2:5]) + merge_high(a[5:8], b[5:8])
+            for k, plane in enumerate(planes):
+                out_ref[k, r : r + 8, c : c + LANES] = plane
+    if edges:
+        edge_rows(list(refs[:-2]) + [out_ref], refs[-1])
+
+
+def final_body(_, near_ref, far_ref, *refs):
     *inputs, out_ref = refs
+    rows = inputs[0].shape[1]
+    at = 0
     for piece in range(len(inputs) // 2):
         own_ref, other_ref = inputs[2 * piece : 2 * piece + 2]
-        _, rows, cols = own_ref.shape
-        for r in range(0, rows, 8):
-            for c in range(0, cols, LANES):
-                a = [own_ref[k, r : r + 8, c : c + LANES] for k in range(8)]
-                b = [other_ref[k, r : r + 8, c : c + LANES] for k in range(8)]
-                total, number = a[0] + b[0], a[1] + b[1]
-                low = merge_low(a[2:5], b[2:5])
-                high = merge_high(a[5:8], b[5:8])
-                at = piece * cols + c
-                if last:
-                    low_sum = low[0] + low[1] + low[2]
-                    high_sum = high[0] + high[1] + high[2]
-                    out_ref[r : r + 8, at : at + LANES] = (total - low_sum - high_sum) / (number - 6.0)
-                else:
-                    for k, plane in enumerate((total, number) + low + high):
-                        out_ref[k, r : r + 8, at : at + LANES] = plane
-
-
-def join_body(swap_cols, own_ref, pair_ref, a_same, a_cross, b_same, b_cross, coadd_ref, rim_ref, *outs):
+        for c in range(0, own_ref.shape[2], LANES):
+            here = slice(at, at + LANES)
+            at += LANES
+            for r in range(0, rows, 8):
+                both = [[ref[k, r : r + 8, c : c + LANES] for k in range(8)] for ref in (own_ref, other_ref)]
+                out_ref[r : r + 8, here] = finish(*both)
+            both = [
+                [pltpu.roll(ref[k // 2 * 8 : k // 2 * 8 + 8, here], RIM, 0) if k % 2 else ref[k // 2 * 8 : k // 2 * 8 + 8, here] for k in range(8)]
+                for ref in (near_ref, far_ref)
+            ]
+            value = finish(*both)
+            out_ref[rows : rows + 8, here] = jnp.where(odd_tile(), value, pltpu.roll(value, RIM, 0))
+
+
+def join_body(swap_cols, own_ref, pair_ref, coadd_ref, rim_ref, *outs):
     above, below, left, right = sides()
-    parity = (lax.axis_index("exp") + lax.axis_index("strip")) % 2
-    even = parity == 0
+    even = ~odd_tile()
     own, pair = own_ref[...], pair_ref[...]
-    n, cols = own.shape
-    coadd_ref[:n, :] = jnp.where(even, own, pair)
-    coadd_ref[n:, :] = jnp.where(even, pair, own)
+    n, cols = own.shape[0] - 8, own.shape[1]
+    first, last = jnp.where(even, own, pair), jnp.where(even, pair, own)
+    coadd_ref[:n, :] = first[:n]
+    coadd_ref[n:, :] = last[:n]
     sub = iota((8, cols), 0)
-    low = jnp.where(even, b_cross[:8, :], b_same[:8, :])
-    high = jnp.where(even, a_same[n - 8 :, :], a_cross[n - 8 :, :])
-    rim_ref[...] = jnp.where(sub < RIM, jnp.where(below, low, 0.0), jnp.where(above, high, 0.0))
+    rim_ref[...] = jnp.where(sub < RIM, jnp.where(below, last[n:], 0.0), jnp.where(above, first[n:], 0.0))
     for ref, at in ((coadd_ref, 0), (rim_ref, 2 * n)):
         rows = ref.shape[0]
         lefts, rights = ref[:, :LANES], ref[:, cols - LANES :]
@@ -404,6 +445,20 @@
                 if 0 <= s_from < sizes[1] and 0 <= b_from < sizes[2]:
                     source = ((z ^ exp_bit) * sizes[1] + s_from) * sizes[2] + b_from
                     pairs.append((source, (z * sizes[1] + s) * sizes[2] + b))
+    return lax.ppermute(value, ("exp", "strip", "band"), pairs)
+
+
+def facing(value, exp_bit):
+    sizes = [lax.axis_size(a) for a in ("exp", "strip", "band")]
+    pairs = []
+    for z in range(sizes[0]):
+        for s in range(sizes[1]):
+            s_from = s + (1 if (z + s) % 2 else -1)
+            if sizes[1] % 2 == 0:
+                s_from %= sizes[1]
+            if 0 <= s_from < sizes[1]:
+                for b in range(sizes[2]):
+                    pairs.append((((z ^ exp_bit) * sizes[1] + s_from) * sizes[2] + b, (z * sizes[1] + s) * sizes[2] + b))
     return lax.ppermute(value, ("exp", "strip", "band"), pairs)
 
 
@@ -467,12 +522,21 @@
 
     sents = [moved(warp(True, piece), 1, 0, 0) for piece in pieces]
     own = warp(False, blocks)
-    states = [
-        call(functools.partial(gather_body, LANES * piece[0]), f32(8, *sent.shape[1:]), [VMEM, VMEM], area * 100, 400000)(
-            own, sent
-        )
-        for piece, sent in zip(pieces, sents)
-    ]
+    edge_out = f32(8 * RIM, cols)
+    states = []
+    for piece, sent in zip(pieces, sents):
+        edges = layers == 4 and piece is pieces[-1]
+        outs = f32(8, *sent.shape[1:])
+        done = call(
+            functools.partial(gather_body, LANES * piece[0], edges),
+            [outs, edge_out] if edges else outs,
+            [VMEM] * (2 + len(states) * edges),
+            area * 100,
+            400000,
+        )(own, sent, *(states if edges else []))
+        states.append(done[0] if edges else done)
+        if edges:
+            edge_state = done[1]
     match_taps = call(
         match_taps_body,
         jax.ShapeDtypeStruct((tiles, 4 * TILE_ROWS * count, DEPTH), half),
@@ -482,31 +546,38 @@
         scratch(2 * TILE_ROWS),
     )(psf_bank, turned(match_index), states[0])
     bit = 2
-    while bit < layers:
+    while 2 * bit < layers:
         others = [moved(state, bit, 0, 0) for state in states]
-        if 2 * bit == layers:
-            groups = [[x for both in zip(states, others) for x in both]]
-            outs = [f32(TILE_ROWS, cols)]
-        else:
-            groups = [list(both) for both in zip(states, others)]
-            outs = [f32(*state.shape) for state in states]
-        states = [
-            call(functools.partial(merge_body, 2 * bit == layers), out, [pl.BlockSpec(memory_space=pl.ANY)] + [VMEM] * len(group), area * 20, 300000)(match_taps, *group)
-            for out, group in zip(outs, groups)
-        ]
+        before, states = states, []
+        for own_state, other in zip(before, others):
+            edges = 4 * bit == layers and own_state is before[-1]
+            outs = f32(*other.shape)
+            done = call(
+                functools.partial(merge_body, edges),
+                [outs, edge_out] if edges else outs,
+                [VMEM] * (2 + len(states) * edges),
+                area * 20,
+                300000,
+            )(own_state, other, *(states if edges else []))
+            states.append(done[0] if edges else done)
+            if edges:
+                edge_state = done[1]
         bit *= 2
-    (state,) = states
+    others = [moved(state, bit, 0, 0) for state in states]
+    near, far = facing(edge_state, 0), facing(edge_state, bit)
+    group = [x for both in zip(states, others) for x in both]
+    state = call(
+        final_body,
+        f32(TILE_ROWS + 8, cols),
+        [pl.BlockSpec(memory_space=pl.ANY)] + [VMEM] * (2 + len(group)),
+        area * 20,
+        300000,
+    )(match_taps, near, far, *group)
     pair = moved(state, 1, 0, 0)
-    if swap_rows:
-        same = moved(state, 0, 1, 0)
-        cross = moved(state, 1, 1, 0)
-        near = (same, cross, same, cross)
-    else:
-        near = (moved(state, 0, -1, 0), moved(state, 1, -1, 0), moved(state, 0, 1, 0), moved(state, 1, 1, 0))
     side_outs = [f32(rows + 8, LANES)] * (1 if swap_cols else 2)
     coadd, rim, *side = call(
-        functools.partial(join_body, swap_cols), [f32(rows, cols), f32(8, cols)] + side_outs, [VMEM] * 6, 10000, 100000
-    )(state, pair, *near)
+        functools.partial(join_body, swap_cols), [f32(rows, cols), f32(8, cols)] + side_outs, [VMEM] * 2, 10000, 100000
+    )(state, pair)
     if swap_cols:
         left = right = moved(side[0], 0, 0, 1)
     else:

time: 31.2 us -> 30.2 us (0.968)
  waiting for transfers between devices: 9.28 us -> 7.51 us
  starting transfers between devices: 13.5 us -> 14.3 us
    ppermute x11 -> x9, waiting for transfers between devices: 9.28 us -> 5.52 us  [moved(): return lax.ppermute(value, ('exp', 'strip', 'band'), pairs)]
    ppermute x0 -> x2, starting transfers between devices: none -> 2.58 us  [facing(): return lax.ppermute(value, ('exp', 'strip', 'band'), pairs)]
    ppermute x0 -> x2, waiting for transfers between devices: none -> 1.99 us  [facing(): return lax.ppermute(value, ('exp', 'strip', 'band'), pairs)]
    ppermute x11 -> x9, starting transfers between devices: 13.5 us -> 11.7 us  [moved(): return lax.ppermute(value, ('exp', 'strip', 'band'), pairs)]
  transfers between devices with their start and end apart: 11 -> 11, of which waited for: 7 -> 5; matrix products, arithmetic and copies ran while one was open for 0% -> 0% of each run, Pallas kernels for 13% -> 13%
where the time goes in v3:
time: 30.2 us; the launch traced here: 30.1 us
  starting transfers between devices  14.3 us (47%)
  waiting for transfers between devices  7.51 us (25%)
  Pallas kernels  6.09 us (20%)
  local copies, waits for them, and re-layouts  1.44 us (5%)
  between operations  0.74 us (2%)
    ppermute x9, starting transfers between devices, moved(): return lax.ppermute(value, ('exp', 'strip', 'band'), pairs)  11.7 us
    ppermute x9, waiting for transfers between devices, moved(): return lax.ppermute(value, ('exp', 'strip', 'band'), pairs)  5.52 us
    ppermute x2, starting transfers between devices, facing(): return lax.ppermute(value, ('exp', 'strip', 'band'), pairs)  2.58 us
    ppermute x2, waiting for transfers between devices, facing(): return lax.ppermute(value, ('exp', 'strip', 'band'), pairs)  1.99 us
    pallas_call x3, Pallas kernels, warp(): call(functools.partial(warp_body, sent, piece), f32(count, TILE_ROWS, LAN...  1.87 us
    unnamed x12, local copies, waits for them, and re-layouts  1.44 us
    pallas_call x1, Pallas kernels, on_device(): pl.pallas_call(match_body, out_shape=[f32(rows, cols), f32(count, rows, c...  1.44 us
    pallas_call x1, Pallas kernels, on_device(): call(warp_taps_body, jax.ShapeDtypeStruct((tiles, count, 2 * GROUP * TILE...  1.32 us
  transfers between devices with their start and end apart: 11, of which 5 were waited for; matrix products, arithmetic and copies ran while one was open for 0% of the time, Pallas kernels for 13%

profile of v3, /device:TPU:0, one launch (start us, length us, event | category | flops | bytes accessed | tf_op | source)
XLA Modules:
  0.0 30.1 jit_solution(17099282868738515750)
XLA Ops:
  0.6 0.9 %copy-done = f32[8,32,256]{2,1,0:T(8,128)S(1)} copy-done((f32[8,32,256]{2,1,0:T(8,128)S(1)}, f32[8,32,256]{2,1,0:T(8,128)}, u32[]{:S(2)}) %copy-start) | copy-done | bytes 262168
  1.6 0.1 shard_map.69
  1.7 3.0 %collective-permute-start = (f32[32,256]{1,0:T(8,128)S(1)}, f32[32,256]{1,0:T(8,128)S(1)}, u32[]{:S(2)}, u32[]{:S(2)}) collective-permute-start(f32[32,256]{1,0:T(8,128)S(1)} %get-tuple-element.10), channel_id=1, source_target_pairs={{2,0},{3,1},{0,2},{1,3},{6,4},{7,5},{4,6},{5,7},{10,8},{11,9},{8,1... | collective-permute-start | bytes 98312 | tf_op jit(solution)/shard_map/ppermute | solution.py:448
  4.8 0.2 collective-permute-start.2
  5.0 0.5 %copy-done.4 = s32[8,2,2]{0,2,1:T(2,128)S(1)} copy-done((s32[8,2,2]{0,2,1:T(2,128)S(1)}, s32[8,2,2]{0,2,1:T(2,128)}, u32[]{:S(2)}) %copy-start.4) | copy-done | bytes 152
  5.4 1.3 %shard_map.68.taps_ref = bf16[2,8,96,256]{3,2,1,0:T(8,128)(2,1)S(1)} custom-call(f32[16,81]{1,0:T(8,128)S(1)} %copy-done.3, s32[2,2,8]{2,1,0:T(2,128)S(1)} %bitcast.2), custom_call_target="tpu_custom_call" | custom-call | flops 10000000 | bytes 300000 | tf_op jit(solution)/shard_map/pallas_call | solution.py:502
  6.8 1.0 %collective-permute-done.2.c_al.c_ar.c_bl.c_br = f32[8,128]{1,0:T(8,128)S(1)} collective-permute-done((f32[8,128]{1,0:T(8,128)S(1)}, f32[8,128]{1,0:T(8,128)S(1)}, u32[]{:S(2)}, u32[]{:S(2)}) %collective-permute-start.2) | collective-permute-done | bytes 4128 | tf_op jit(solution)/shard_map/ppermute | solution.py:448
  7.8 0.6 %shard_map.71 = f32[8,16,128]{2,1,0:T(8,128)S(1)} custom-call(f32[8,32,256]{2,1,0:T(8,128)S(1)} %copy-done.1, s32[8,32,256]{2,1,0:T(8,128)S(1)} %copy-done.2, bf16[2,8,96,256]{3,2,1,0:T(8,128)(2,1)S(1)} %shard_map.68.taps_ref, f32[32,256]{1,0:T(8,128)S(1)} %collective-permute-done.above_ref.below_ref, ...), custom_call_target="tpu_custom_call" | custom-call | flops 100663296 | bytes 1000000 | tf_op jit(solution)/shard_map/pallas_call | solution.py:515
  8.4 1.6 %collective-permute-start.3 = (f32[8,16,128]{2,1,0:T(8,128)S(1)}, f32[8,16,128]{2,1,0:T(8,128)S(1)}, u32[]{:S(2)}, u32[]{:S(2)}) collective-permute-start(f32[8,16,128]{2,1,0:T(8,128)S(1)} %shard_map.71), channel_id=1, source_target_pairs={{4,0},{5,1},{6,2},{7,3},{0,4},{1,5},{2,6},{3,7},{12,8},{13,9},{14,... | collective-permute-start | bytes 196616 | tf_op jit(solution)/shard_map/ppermute | solution.py:448
  10.0 0.6 %shard_map.74 = f32[8,16,128]{2,1,0:T(8,128)S(1)} custom-call(f32[8,32,256]{2,1,0:T(8,128)S(1)} %copy-done.1, s32[8,32,256]{2,1,0:T(8,128)S(1)} %copy-done.2, bf16[2,8,96,256]{3,2,1,0:T(8,128)(2,1)S(1)} %shard_map.68.taps_ref, f32[32,256]{1,0:T(8,128)S(1)} %collective-permute-done.above_ref.below_ref, ...), custom_call_target="tpu_custom_call" | custom-call | flops 100663296 | bytes 1000000 | tf_op jit(solution)/shard_map/pallas_call | solution.py:515
  10.6 0.5 %collective-permute-start.4 = (f32[8,16,128]{2,1,0:T(8,128)S(1)}, f32[8,16,128]{2,1,0:T(8,128)S(1)}, u32[]{:S(2)}, u32[]{:S(2)}) collective-permute-start(f32[8,16,128]{2,1,0:T(8,128)S(1)} %shard_map.74), channel_id=1, source_target_pairs={{4,0},{5,1},{6,2},{7,3},{0,4},{1,5},{2,6},{3,7},{12,8},{13,9},{14,... | collective-permute-start | bytes 196616 | tf_op jit(solution)/shard_map/ppermute | solution.py:448
  11.1 0.7 %shard_map.70.own_ref = f32[8,16,256]{2,1,0:T(8,128)S(1)} custom-call(f32[8,32,256]{2,1,0:T(8,128)S(1)} %copy-done.1, s32[8,32,256]{2,1,0:T(8,128)S(1)} %copy-done.2, bf16[2,8,96,256]{3,2,1,0:T(8,128)(2,1)S(1)} %shard_map.68.taps_ref, f32[32,256]{1,0:T(8,128)S(1)} %collective-permute-done.above_ref.below_ref, ...), custom_call_target="tpu_custom_call" | custom-call | flops 201326592 | bytes 1000000 | tf_op jit(solution)/shard_map/pallas_call | solution.py:515
  11.9 1.1 %collective-permute-done.3.other_ref = f32[8,16,128]{2,1,0:T(8,128)S(1)} collective-permute-done((f32[8,16,128]{2,1,0:T(8,128)S(1)}, f32[8,16,128]{2,1,0:T(8,128)S(1)}, u32[]{:S(2)}, u32[]{:S(2)}) %collective-permute-start.3) | collective-permute-done | bytes 65568 | tf_op jit(solution)/shard_map/ppermute | solution.py:448
  13.0 0.1 shard_map.72._.refs_0_
  13.1 2.7 %collective-permute-start.7 = (f32[8,16,128]{2,1,0:T(8,128)S(1)}, f32[8,16,128]{2,1,0:T(8,128)S(1)}, u32[]{:S(2)}, u32[]{:S(2)}) collective-permute-start(f32[8,16,128]{2,1,0:T(8,128)S(1)} %shard_map.72._.refs_0_), channel_id=1, source_target_pairs={{8,0},{9,1},{10,2},{11,3},{12,4},{13,5},{14,6},{15,7},{0,8},{1,9},... | collective-permute-start | bytes 196616 | tf_op jit(solution)/shard_map/ppermute | solution.py:448
  15.8 1.9 %collective-permute-start.8 = (f32[8,16,128]{2,1,0:T(8,128)S(1)}, f32[8,16,128]{2,1,0:T(8,128)S(1)}, u32[]{:S(2)}, u32[]{:S(2)}) collective-permute-start(f32[8,16,128]{2,1,0:T(8,128)S(1)} %get-tuple-element.14.refs_2_), channel_id=1, source_target_pairs={{8,0},{9,1},{10,2},{11,3},{12,4},{13,5},{14,6},{15,7},{0,8},{1,9},... | collective-permute-start | bytes 196616 | tf_op jit(solution)/shard_map/ppermute | solution.py:448
  17.7 1.2 %collective-permute-start.6 = (f32[32,256]{1,0:T(8,128)S(1)}, f32[32,256]{1,0:T(8,128)S(1)}, u32[]{:S(2)}, u32[]{:S(2)}) collective-permute-start(f32[32,256]{1,0:T(8,128)S(1)} %get-tuple-element.13), channel_id=1, source_target_pairs={{10,0},{11,1},{8,2},{9,3},{14,4},{15,5},{12,6},{13,7},{2,8},{3,9},... | collective-permute-start | bytes 98312 | tf_op jit(solution)/shard_map/ppermute | solution.py:462
  18.9 1.4 %collective-permute-start.5 = (f32[32,256]{1,0:T(8,128)S(1)}, f32[32,256]{1,0:T(8,128)S(1)}, u32[]{:S(2)}, u32[]{:S(2)}) collective-permute-start(f32[32,256]{1,0:T(8,128)S(1)} %get-tuple-element.13), channel_id=1, source_target_pairs={{2,0},{3,1},{0,2},{1,3},{6,4},{7,5},{4,6},{5,7},{10,8},{11,9},{8,1... | collective-permute-start | bytes 98312 | tf_op jit(solution)/shard_map/ppermute | solution.py:462
  20.3 1.1 %shard_map.73._.taps_ref = bf16[2,512,256]{2,1,0:T(8,128)(2,1)S(1)} custom-call(f32[16,81]{1,0:T(8,128)S(1)} %copy-done.3, s32[2,2,8]{2,1,0:T(2,128)S(1)} %bitcast.3, f32[8,16,128]{2,1,0:T(8,128)S(1)} %shard_map.72._.refs_0_), custom_call_target="tpu_custom_call" | custom-call | flops 10000000 | bytes 300000 | tf_op jit(solution)/shard_map/pallas_call | solution.py:540
  21.4 2.0 %collective-permute-done.6.far_ref = f32[32,256]{1,0:T(8,128)S(1)} collective-permute-done((f32[32,256]{1,0:T(8,128)S(1)}, f32[32,256]{1,0:T(8,128)S(1)}, u32[]{:S(2)}, u32[]{:S(2)}) %collective-permute-start.6) | collective-permute-done | bytes 32800 | tf_op jit(solution)/shard_map/ppermute | solution.py:462
  23.4 1.7 %collective-permute-start.9 = (f32[24,256]{1,0:T(8,128)S(1)}, f32[24,256]{1,0:T(8,128)S(1)}, u32[]{:S(2)}, u32[]{:S(2)}) collective-permute-start(f32[24,256]{1,0:T(8,128)S(1)} %shard_map.76.own_ref), channel_id=1, source_target_pairs={{4,0},{5,1},{6,2},{7,3},{0,4},{1,5},{2,6},{3,7},{12,8},{13,9},{14,... | collective-permute-start | bytes 73736 | tf_op jit(solution)/shard_map/ppermute | solution.py:448
  25.1 2.2 %collective-permute-done.9.pair_ref = f32[24,256]{1,0:T(8,128)S(1)} collective-permute-done((f32[24,256]{1,0:T(8,128)S(1)}, f32[24,256]{1,0:T(8,128)S(1)}, u32[]{:S(2)}, u32[]{:S(2)}) %collective-permute-start.9) | collective-permute-done | bytes 24608 | tf_op jit(solution)/shard_map/ppermute | solution.py:448
  27.4 1.2 %collective-permute-done.10.left_ref.right_ref = f32[40,128]{1,0:T(8,128)S(1)} collective-permute-done((f32[40,128]{1,0:T(8,128)S(1)}, f32[40,128]{1,0:T(8,128)S(1)}, u32[]{:S(2)}, u32[]{:S(2)}) %collective-permute-start.10) | collective-permute-done | bytes 20512 | tf_op jit(solution)/shard_map/ppermute | solution.py:448
  28.6 1.4 %shard_map.78 = (f32[32,256]{1,0:T(8,128)}, f32[8,32,256]{2,1,0:T(8,128)}) custom-call(f32[8,32,256]{2,1,0:T(8,128)S(1)} %copy-done.1, bf16[2,512,256]{2,1,0:T(8,128)(2,1)S(1)} %shard_map.73._.taps_ref, f32[32,256]{1,0:T(8,128)S(1)} %get-tuple-element.15.coadd_ref, f32[8,256]{1,0:T(8,128)S(1)} %get-tuple-element.16.rim_ref, ...), custom_call_target="tpu_custom_call" | custom-call | flops 134217728 | bytes 1000000 | tf_op jit(solution)/shard_map/pallas_call | solution.py:585
  (21 shorter events, 0.2 us)
Async XLA Ops:
  0.6 1.0 %copy-start = (f32[8,32,256]{2,1,0:T(8,128)S(1)}, f32[8,32,256]{2,1,0:T(8,128)}, u32[]{:S(2)}) copy-start(f32[8,32,256]{2,1,0:T(8,128)} %images_ref.9) | copy-start | bytes 786436
  1.6 3.4 %copy-start.3 = (f32[16,81]{1,0:T(8,128)S(1)}, f32[16,81]{1,0:T(8,128)}, u32[]{:S(2)}) copy-start(f32[16,81]{1,0:T(8,128)} %bank_ref.3) | copy-start | bytes 15556
  1.7 6.1 %collective-permute-start = (f32[32,256]{1,0:T(8,128)S(1)}, f32[32,256]{1,0:T(8,128)S(1)}, u32[]{:S(2)}, u32[]{:S(2)}) collective-permute-start(f32[32,256]{1,0:T(8,128)S(1)} %get-tuple-element.10), channel_id=1, source_target_pairs={{2,0},{3,1},{0,2},{1,3},{6,4},{7,5},{4,6},{5,7},{10,8},{11,9},{8,1... | collective-permute-start | bytes 98312 | tf_op jit(solution)/shard_map/ppermute | solution.py:448
  4.8 0.7 %copy-start.4 = (s32[8,2,2]{0,2,1:T(2,128)S(1)}, s32[8,2,2]{0,2,1:T(2,128)}, u32[]{:S(2)}) copy-start(s32[8,2,2]{0,2,1:T(2,128)} %param.7) | copy-start | bytes 388
  4.8 3.0 %collective-permute-start.1 = (f32[32,128]{1,0:T(8,128)S(1)}, f32[32,128]{1,0:T(8,128)S(1)}, u32[]{:S(2)}, u32[]{:S(2)}) collective-permute-start(f32[32,128]{1,0:T(8,128)S(1)} %get-tuple-element.11), channel_id=1, source_target_pairs={{1,0},{0,1},{3,2},{2,3},{5,4},{4,5},{7,6},{6,7},{9,8},{8,9},{11,10... | collective-permute-start | bytes 49160 | tf_op jit(solution)/shard_map/ppermute | solution.py:448
  4.8 3.0 %collective-permute-start.2 = (f32[8,128]{1,0:T(8,128)S(1)}, f32[8,128]{1,0:T(8,128)S(1)}, u32[]{:S(2)}, u32[]{:S(2)}) collective-permute-start(f32[8,128]{1,0:T(8,128)S(1)} %get-tuple-element.12), channel_id=1, source_target_pairs={{3,0},{2,1},{1,2},{0,3},{7,4},{6,5},{5,6},{4,7},{11,8},{10,9},{9,1... | collective-permute-start | bytes 12296 | tf_op jit(solution)/shard_map/ppermute | solution.py:448
  5.4 2.4 %copy-start.1 = (f32[8,32,256]{2,1,0:T(8,128)S(1)}, f32[8,32,256]{2,1,0:T(8,128)}, u32[]{:S(2)}) copy-start(f32[8,32,256]{2,1,0:T(8,128)} %images_ref.9) | copy-start | bytes 786436
  5.4 2.4 %copy-start.2 = (s32[8,32,256]{2,1,0:T(8,128)S(1)}, s32[8,32,256]{2,1,0:T(8,128)}, u32[]{:S(2)}) copy-start(s32[8,32,256]{2,1,0:T(8,128)} %mask_ref.5) | copy-start | bytes 786436
  8.4 4.6 %collective-permute-start.3 = (f32[8,16,128]{2,1,0:T(8,128)S(1)}, f32[8,16,128]{2,1,0:T(8,128)S(1)}, u32[]{:S(2)}, u32[]{:S(2)}) collective-permute-start(f32[8,16,128]{2,1,0:T(8,128)S(1)} %shard_map.71), channel_id=1, source_target_pairs={{4,0},{5,1},{6,2},{7,3},{0,4},{1,5},{2,6},{3,7},{12,8},{13,9},{14,... | collective-permute-start | bytes 196616 | tf_op jit(solution)/shard_map/ppermute | solution.py:448
  10.6 5.1 %collective-permute-start.4 = (f32[8,16,128]{2,1,0:T(8,128)S(1)}, f32[8,16,128]{2,1,0:T(8,128)S(1)}, u32[]{:S(2)}, u32[]{:S(2)}) collective-permute-start(f32[8,16,128]{2,1,0:T(8,128)S(1)} %shard_map.74), channel_id=1, source_target_pairs={{4,0},{5,1},{6,2},{7,3},{0,4},{1,5},{2,6},{3,7},{12,8},{13,9},{14,... | collective-permute-start | bytes 196616 | tf_op jit(solution)/shard_map/ppermute | solution.py:448
  13.1 10.3 %collective-permute-start.7 = (f32[8,16,128]{2,1,0:T(8,128)S(1)}, f32[8,16,128]{2,1,0:T(8,128)S(1)}, u32[]{:S(2)}, u32[]{:S(2)}) collective-permute-start(f32[8,16,128]{2,1,0:T(8,128)S(1)} %shard_map.72._.refs_0_), channel_id=1, source_target_pairs={{8,0},{9,1},{10,2},{11,3},{12,4},{13,5},{14,6},{15,7},{0,8},{1,9},... | collective-permute-start | bytes 196616 | tf_op jit(solution)/shard_map/ppermute | solution.py:448
  15.8 4.5 %copy-start.5 = (s32[8,2,2]{0,2,1:T(2,128)S(1)}, s32[8,2,2]{0,2,1:T(2,128)}, u32[]{:S(2)}) copy-start(s32[8,2,2]{0,2,1:T(2,128)} %param.8) | copy-start | bytes 388
  15.8 7.6 %collective-permute-start.8 = (f32[8,16,128]{2,1,0:T(8,128)S(1)}, f32[8,16,128]{2,1,0:T(8,128)S(1)}, u32[]{:S(2)}, u32[]{:S(2)}) collective-permute-start(f32[8,16,128]{2,1,0:T(8,128)S(1)} %get-tuple-element.14.refs_2_), channel_id=1, source_target_pairs={{8,0},{9,1},{10,2},{11,3},{12,4},{13,5},{14,6},{15,7},{0,8},{1,9},... | collective-permute-start | bytes 196616 | tf_op jit(solution)/shard_map/ppermute | solution.py:448
  17.7 5.7 %collective-permute-start.6 = (f32[32,256]{1,0:T(8,128)S(1)}, f32[32,256]{1,0:T(8,128)S(1)}, u32[]{:S(2)}, u32[]{:S(2)}) collective-permute-start(f32[32,256]{1,0:T(8,128)S(1)} %get-tuple-element.13), channel_id=1, source_target_pairs={{10,0},{11,1},{8,2},{9,3},{14,4},{15,5},{12,6},{13,7},{2,8},{3,9},... | collective-permute-start | bytes 98312 | tf_op jit(solution)/shard_map/ppermute | solution.py:462
  18.9 4.5 %collective-permute-start.5 = (f32[32,256]{1,0:T(8,128)S(1)}, f32[32,256]{1,0:T(8,128)S(1)}, u32[]{:S(2)}, u32[]{:S(2)}) collective-permute-start(f32[32,256]{1,0:T(8,128)S(1)} %get-tuple-element.13), channel_id=1, source_target_pairs={{2,0},{3,1},{0,2},{1,3},{6,4},{7,5},{4,6},{5,7},{10,8},{11,9},{8,1... | collective-permute-start | bytes 98312 | tf_op jit(solution)/shard_map/ppermute | solution.py:462
  23.4 3.9 %collective-permute-start.9 = (f32[24,256]{1,0:T(8,128)S(1)}, f32[24,256]{1,0:T(8,128)S(1)}, u32[]{:S(2)}, u32[]{:S(2)}) collective-permute-start(f32[24,256]{1,0:T(8,128)S(1)} %shard_map.76.own_ref), channel_id=1, source_target_pairs={{4,0},{5,1},{6,2},{7,3},{0,4},{1,5},{2,6},{3,7},{12,8},{13,9},{14,... | collective-permute-start | bytes 73736 | tf_op jit(solution)/shard_map/ppermute | solution.py:448
  27.4 1.3 %collective-permute-start.10 = (f32[40,128]{1,0:T(8,128)S(1)}, f32[40,128]{1,0:T(8,128)S(1)}, u32[]{:S(2)}, u32[]{:S(2)}) collective-permute-start(f32[40,128]{1,0:T(8,128)S(1)} %get-tuple-element.17), channel_id=1, source_target_pairs={{1,0},{0,1},{3,2},{2,3},{5,4},{4,5},{7,6},{6,7},{9,8},{8,9},{11,10... | collective-permute-start | bytes 61448 | tf_op jit(solution)/shard_map/ppermute | solution.py:448
